TPU v7x, 256 devices: a whole 4x4x8 slice. The times are simulated.
256 devices in a mesh: segment: 2 (over x_lo), win: 32 (over x_hi, z, core), mp: 4 (over y).
Axes of the slice: x: 4 (x_hi: 2, x_lo: 2; x = x_hi * 2 + x_lo), y: 4, z: 8, core: 2. Of those that a mesh axis runs over, the one named last changes fastest.
Arguments:
- feats: bfloat16 [32, 1536, 256], P('win'), may hold values from -6 to 6
- convolution_kernel_weight: bfloat16 [1536, 5, 1536], P('win', None, 'mp'), may hold values from -0.0625 to 0.0625
- conv_bias: float32 [1536], P('mp'), may hold values from -3 to 3
- qkv_weight: bfloat16 [1536, 2560], P('win', 'mp'), may hold values from -0.15625 to 0.15625
- out_weight: bfloat16 [1536, 1536], P('win', 'mp'), may hold values from -0.15625 to 0.15625
- head_weight: bfloat16 [1536, 4096], P('win', 'mp'), may hold values from -0.15625 to 0.15625
- head_bias: float32 [4096], P('mp'), may hold values from -4 to 4
- exon_lists: int32 [3, 32, 64, 8], P(None, 'win'), may hold values from 0 to 256, as said below
Outputs:
- gene_tracks: float32 [512, 4096], P(('segment', 'win'), 'mp')
Inputs may be any that keep to these rules, and one draw needn't show every extreme that they name: `exon_lists`: A slot with equal first and end bin is unused and has gene slot 0; used slots have 1 to 8 bins and a gene slot below 8. In every draw some owners receive 8 used ranges from every window.
All inputs are finite; a program needn't handle non-finite values.
Results may differ from a plain program's by a relative error of at most 0.0025.
Values may be sent and summed in bfloat16 or wider, within the bound.
A program may use at most 64 MiB of HBM per device.

v0:
```python
import math

import jax
import jax.numpy as jnp
from jax import lax
from jax.sharding import PartitionSpec as P

KEY = 64
VAL = 192
DILATION_STEP = 4
GENE_DEV = 8


def passed_along(x, axis, by):
    devices = lax.axis_size(axis)
    pairs = [(i, i + by) for i in range(devices) if 0 <= i + by < devices]
    return lax.ppermute(x, axis, pairs)


def contract_rows(left, right):
    return lax.dot_general(
        left, right, (((0,), (0,)), ((), ())), preferred_element_type=jnp.float32
    )


def conv_terms(piece, padded_input, window_bin_count):
    running = contract_rows(piece[:, 0, :], padded_input[:, 0:window_bin_count])
    for tap_index in range(1, piece.shape[1]):
        shifted_input = padded_input[
            :, tap_index * DILATION_STEP : tap_index * DILATION_STEP + window_bin_count
        ]
        running = running + contract_rows(piece[:, tap_index, :], shifted_input)
    return running


def make_section_collect(padded_input, window_bin_count, conv_segment, tap_count, out_cols):

    def collect(carried, piece, offset_row):
        conv_acc, packed_full = carried
        conv_piece = piece[:, : tap_count * out_cols].reshape(piece.shape[0], tap_count, out_cols)
        conv_acc = lax.cond(
            conv_segment,
            lambda running: conv_terms(conv_piece, padded_input, window_bin_count),
            lambda running: running,
            conv_acc,
        )
        packed_full = piece
        return (conv_acc, packed_full)

    return collect


def attend(all_chan, qkv_full):
    qkv_rows = contract_rows(qkv_full, all_chan).astype(jnp.bfloat16)
    head_span = 2 * KEY + VAL
    score_scale = 1.0 / math.sqrt(KEY)
    outputs = []
    for head_idx in range(qkv_full.shape[1] // head_span):
        offset = head_idx * head_span
        query_rows = qkv_rows[offset : offset + KEY]
        key_rows = qkv_rows[offset + KEY : offset + 2 * KEY]
        value_rows = qkv_rows[offset + 2 * KEY : offset + head_span]
        scores = contract_rows(query_rows, key_rows) * score_scale
        weights = jnp.exp(scores)
        prob_rows = (weights / jnp.sum(weights, axis=1, keepdims=True)).astype(jnp.bfloat16)
        head_out = lax.dot_general(
            value_rows, prob_rows, (((1,), (1,)), ((), ())), preferred_element_type=jnp.float32
        )
        outputs.append(head_out.astype(jnp.bfloat16))
    return jnp.concatenate(outputs, axis=0)


def project(out_full, joined):
    return lax.dot_general(
        out_full, joined, (((1,), (0,)), ((), ())), preferred_element_type=jnp.float32
    )


def gene_entries(resid, head_full, bias_cols, ranges):
    logits = contract_rows(head_full, resid) + bias_cols[:, None]
    tracks = jax.nn.softplus(logits).astype(jnp.bfloat16)
    position = jnp.arange(resid.shape[1], dtype=jnp.int32)
    starts = ranges[0].reshape(-1)
    end_bins = ranges[1].reshape(-1)
    inside = (position[None, :] >= starts[:, None]) & (position[None, :] < end_bins[:, None])
    return lax.dot_general(
        inside.astype(jnp.bfloat16),
        tracks,
        (((1,), (1,)), ((), ())),
        preferred_element_type=jnp.float32,
    )


def local(
    feats,
    convolution_kernel_weight,
    conv_bias,
    qkv_weight,
    out_weight,
    head_weight,
    head_bias,
    exon_lists,
):
    segment_index = lax.axis_index("segment")
    model_index = lax.axis_index("mp")
    source = feats[0]
    chan_count, window_bin_count = source.shape
    tap_count = convolution_kernel_weight.shape[1]
    out_cols = convolution_kernel_weight.shape[2]
    receptive_reach_bins = (tap_count - 1) // 2 * DILATION_STEP
    padded_input = jnp.pad(source, ((0, 0), (receptive_reach_bins, receptive_reach_bins)))
    ranges = exon_lists[:, 0]
    owners = ranges.shape[1]
    slot_count = ranges.shape[2]
    slot_ids = jnp.arange(GENE_DEV, dtype=jnp.int32)
    gene_slots = ranges[2].astype(jnp.float32)
    conv_segment = segment_index == 0
    local_rows = convolution_kernel_weight.shape[0]
    conv_flat = convolution_kernel_weight.reshape(local_rows, tap_count * out_cols)
    later_flat = jnp.concatenate([qkv_weight, out_weight, head_weight], axis=1)
    packed_width = max(conv_flat.shape[1], later_flat.shape[1])
    conv_flat = jnp.pad(conv_flat, ((0, 0), (0, packed_width - conv_flat.shape[1])))
    packed = jnp.where(conv_segment, conv_flat, later_flat)
    collect = make_section_collect(
        padded_input, window_bin_count, conv_segment, tap_count, out_cols
    )
    start_state = (
        jnp.zeros((out_cols, window_bin_count), jnp.float32),
        jnp.zeros((chan_count, packed_width), jnp.bfloat16),
    )
    conv_acc, packed_full = collect(
        start_state, lax.all_gather(packed, "win", axis=0, tiled=True), jnp.int32(0)
    )
    qkv_cols = qkv_weight.shape[1]
    proj_cols = out_weight.shape[1]
    track_width = head_weight.shape[1]
    qkv_full = packed_full[:, :qkv_cols]
    out_full = packed_full[:, qkv_cols : qkv_cols + proj_cols]
    head_full = packed_full[:, qkv_cols + proj_cols : qkv_cols + proj_cols + track_width]
    own_rows = lax.dynamic_slice_in_dim(source, model_index * out_cols, out_cols, 0)
    conv_out = (own_rows + jax.nn.gelu(conv_acc + conv_bias[:, None])).astype(jnp.bfloat16)
    handed = passed_along(conv_out, "segment", 1)
    all_chan = lax.all_gather(handed, "mp", axis=0, tiled=True)
    attn_segment = segment_index == 1
    partial_value = lax.cond(
        attn_segment,
        lambda: project(out_full, attend(all_chan, qkv_full)),
        lambda: jnp.zeros((chan_count, window_bin_count), jnp.float32),
    )
    summed = lax.psum(partial_value.astype(jnp.bfloat16), "mp").astype(jnp.float32)
    resid = (all_chan.astype(jnp.float32) + summed).astype(jnp.bfloat16)
    track_cols = head_full.shape[1]
    entries = lax.cond(
        attn_segment,
        lambda: gene_entries(resid, head_full, head_bias, ranges),
        lambda: jnp.zeros((owners * slot_count, track_cols), jnp.float32),
    )
    entry_rows = entries.reshape(owners, slot_count, track_cols)
    got_rows, got_slots = (
        lax.all_to_all(
            entry_rows.astype(jnp.bfloat16),
            ("segment", "win"),
            split_axis=0,
            concat_axis=0,
            tiled=True,
        ).astype(entry_rows.dtype),
        lax.all_to_all(
            gene_slots.astype(jnp.bfloat16),
            ("segment", "win"),
            split_axis=0,
            concat_axis=0,
            tiled=True,
        ).astype(gene_slots.dtype),
    )
    onehot = (got_slots.reshape(-1).astype(jnp.int32)[:, None] == slot_ids[None, :]).astype(
        jnp.float32
    )
    gene_sum = lax.dot_general(
        onehot,
        got_rows.reshape(owners * slot_count, track_cols),
        (((0,), (0,)), ((), ())),
        precision=lax.Precision.HIGHEST,
        preferred_element_type=jnp.float32,
    )
    return jnp.log1p(gene_sum)


def solution(mesh):
    in_specs = (
        P("win", None, None),
        P("win", None, "mp"),
        P("mp"),
        P("win", "mp"),
        P("win", "mp"),
        P("win", "mp"),
        P("mp"),
        P(None, "win", None, None),
    )
    out_specs = P(("segment", "win"), "mp")
    return jax.shard_map(local, mesh=mesh, in_specs=in_specs, out_specs=out_specs, check_vma=False)
```

profile of v0, /device:TPU:1, one launch (start us, length us, event | category | flops | bytes accessed | tf_op | source)
XLA Modules:
  0.0 252.6 jit_solution(5097702793287970806)
XLA Ops:
  6.5 0.0 all-gather.2.cloned.1.call-start
  6.5 0.9 copy.53
  7.5 1.6 maximum_select_fusion
  9.1 0.0 all-gather.2.cloned.1.call-update
  9.1 0.0 all-reduce.4.cloned.1.call-start
  9.2 98.8 %all-gather.2.cloned.1.call-done = bf16[1536,2048]{1,0:T(8,128)(2,1)} async-done(((bf16[48,2048]{1,0:T(8,128)(2,1)}), bf16[1536,2048]{1,0:T(8,128)(2,1)}) %all-gather.2.cloned.1.call-update) | async-done | bytes 6291472 | tf_op jit(solution)/shard_map/all_gather | solution.py:132
  107.9 0.0 copy-start.2
  107.9 16.3 %conditional.3 = (f32[384,256]{1,0:T(8,128)S(1)}) conditional(s32[]{:T(128)} %convert_element_type.111, () %tuple.24, (bf16[1,1536,256]{2,1,0:T(8,128)(2,1)}, bf16[1536,2048]{1,0:T(8,128)(2,1)}) %tuple.25), branch_computations={%region_0.1_spmd, %region_1.2_spmd} | conditional | flops 1510342656 | bytes 41680932 | solution.py:41
  108.0 8.6 %copy.46 = bf16[1536,2048]{0,1:T(8,128)(2,1)} copy(bf16[1536,2048]{1,0:T(8,128)(2,1)} %get-tuple-element.63) | data formatting | bytes 12582912 | tf_op jit(solution)/shard_map
  116.6 0.0 copy-start
  116.6 3.1 %slice.75 = bf16[1536,1920]{0,1:T(8,128)(2,1)S(1)} slice(bf16[1536,2048]{0,1:T(8,128)(2,1)} %copy.46), slice={[0:1536], [0:1920]} | slice | bytes 11796480 | tf_op jit(solution)/shard_map/slice | solution.py:40
  119.7 0.0 copy-done
  119.7 0.9 fusion.3
  120.6 0.9 fusion.2
  121.6 0.6 convolution_add_fusion
  122.2 0.9 convolution_bitcast_fusion
  123.1 0.9 fusion.1
  124.1 0.2 copy.52
  124.3 0.0 copy-done.2
  124.3 1.2 fusion.56
  125.4 1.3 collective-permute-start
  126.7 4.2 %collective-permute-done = bf16[384,256]{1,0:T(8,128)(2,1)S(1)} collective-permute-done((bf16[384,256]{1,0:T(8,128)(2,1)S(1)}, bf16[384,256]{1,0:T(8,128)(2,1)S(1)}, u32[]{:S(2)}, u32[]{:S(2)}) %collective-permute-start) | collective-permute-done | bytes 196640 | tf_op jit(solution)/shard_map/ppermute | solution.py:17
  131.0 12.3 %all_gather.7 = bf16[1536,256]{1,0:T(8,128)(2,1)S(1)} all-gather(bf16[384,256]{1,0:T(8,128)(2,1)S(1)} %collective-permute-done), channel_id=1, replica_groups=mesh['segment'=2,'win'=32,'mp'=4] {'mp'}, dimensions={0}, use_global_device_ids=true | all-gather | bytes 983040 | tf_op jit(solution)/shard_map/all_gather | solution.py:143
  143.3 0.0 copy-start.1
  143.3 0.1 conditional.4
  143.3 0.1 broadcast.12
  143.4 0.0 copy-start.3
  143.4 1.2 copy.48
  144.6 0.0 all-reduce.4.cloned.1.call-update
  144.6 0.0 copy-done.1
  144.6 0.7 copy.44
  145.3 14.0 %all-to-all-start = ((bf16[64,1,8]{2,1,0:T(2,128)(2,1)}), bf16[64,1,8]{2,1,0:T(2,128)(2,1)S(1)}, u32[]{:S(2)}, u32[]{:S(2)}) async-start(bf16[64,1,8]{2,1,0:T(2,128)(2,1)} %copy.44), calls=%async_computation | async-start | bytes 65536 | tf_op jit(solution)/shard_map/all_to_all | solution.py:167
  159.3 37.9 %all-reduce.4.cloned.1.call-done = bf16[1536,256]{1,0:T(8,128)(2,1)} async-done(((bf16[1536,256]{1,0:T(8,128)(2,1)}), bf16[1536,256]{1,0:T(8,128)(2,1)}) %all-reduce.4.cloned.1.call-update) | async-done | bytes 786448 | tf_op jit(solution)/shard_map/psum | solution.py:150
  197.3 1.3 add_convert_fusion
  198.6 0.0 copy-done.3
  198.6 1.1 conditional.5
  198.6 1.1 broadcast.14
  199.7 0.0 all-to-all-done
  199.7 16.4 %all-to-all-start.1 = ((bf16[64,8,1024]{2,1,0:T(8,128)(2,1)}), bf16[64,8,1024]{2,1,0:T(8,128)(2,1)S(1)}, u32[]{:S(2)}, u32[]{:S(2)}) async-start(bf16[64,8,1024]{2,1,0:T(8,128)(2,1)} %bitcast.52), calls=%async_computation.1 | async-start | bytes 2097152 | tf_op jit(solution)/shard_map/all_to_all | solution.py:160
  216.2 0.1 convert_reduce_fusion
  216.3 0.1 convert_element_type.107
  216.4 28.3 %all-to-all-done.1 = bf16[64,8,1024]{2,1,0:T(8,128)(2,1)S(1)} async-done(((bf16[64,8,1024]{2,1,0:T(8,128)(2,1)}), bf16[64,8,1024]{2,1,0:T(8,128)(2,1)S(1)}, u32[]{:S(2)}, u32[]{:S(2)}) %all-to-all-start.1) | async-done | bytes 1048608 | tf_op jit(solution)/shard_map/all_to_all | solution.py:160
  244.7 1.0 convolution_log-plus-one_fusion
  (1 shorter events, 0.0 us)
Async XLA Ops:
  6.5 101.4 %all-gather.2.cloned.1.call-start = ((), (), s32[]{:S(2)}) async-start(), calls=%async_computation.2 | async-start | bytes 6488064 | tf_op jit(solution)/shard_map/all_gather | solution.py:132
  9.1 188.1 %all-reduce.4.cloned.1.call-start = ((), (), s32[]{:S(2)}) async-start(), calls=%async_computation.3 | async-start | bytes 1572864 | tf_op jit(solution)/shard_map/psum | solution.py:150
  107.9 16.3 %copy-start.2 = (f32[384]{0:T(512)S(1)}, f32[384]{0:T(512)}, u32[]{:S(2)}) copy-start(f32[384]{0:T(512)} %param.16) | copy-start | bytes 4612
  116.6 3.1 %copy-start = (bf16[1,1536,256]{2,1,0:T(8,128)(2,1)S(1)}, bf16[1,1536,256]{2,1,0:T(8,128)(2,1)}, u32[]{:S(2)}) copy-start(bf16[1,1536,256]{2,1,0:T(8,128)(2,1)} %get-tuple-element.40) | copy-start | bytes 2359300 | tf_op jit(solution)/shard_map/cond
  125.4 5.6 %collective-permute-start = (bf16[384,256]{1,0:T(8,128)(2,1)S(1)}, bf16[384,256]{1,0:T(8,128)(2,1)S(1)}, u32[]{:S(2)}, u32[]{:S(2)}) collective-permute-start(bf16[384,256]{1,0:T(8,128)(2,1)S(1)} %fusion.56), channel_id=1, source_target_pairs={{0,128},{1,129},{2,130},{3,131},{4,132},{5,133},{6,134},{7,135},{8... | collective-permute-start | bytes 589832 | tf_op jit(solution)/shard_map/ppermute | solution.py:17
  143.3 1.3 copy-start.1
  143.4 55.2 %copy-start.3 = (f32[1024]{0:T(1024)S(1)}, f32[1024]{0:T(1024)}, u32[]{:S(2)}) copy-start(f32[1024]{0:T(1024)} %param.20) | copy-start | bytes 12292
  145.3 54.4 %all-to-all-start = ((bf16[64,1,8]{2,1,0:T(2,128)(2,1)}), bf16[64,1,8]{2,1,0:T(2,128)(2,1)S(1)}, u32[]{:S(2)}, u32[]{:S(2)}) async-start(bf16[64,1,8]{2,1,0:T(2,128)(2,1)} %copy.44), calls=%async_computation | async-start | bytes 65536 | tf_op jit(solution)/shard_map/all_to_all | solution.py:167
  199.7 45.0 %all-to-all-start.1 = ((bf16[64,8,1024]{2,1,0:T(8,128)(2,1)}), bf16[64,8,1024]{2,1,0:T(8,128)(2,1)S(1)}, u32[]{:S(2)}, u32[]{:S(2)}) async-start(bf16[64,8,1024]{2,1,0:T(8,128)(2,1)} %bitcast.52), calls=%async_computation.1 | async-start | bytes 2097152 | tf_op jit(solution)/shard_map/all_to_all | solution.py:160
Sparse Core Ops, SparseCore 0:
  10.1 97.8 all-gather.1
  144.7 52.4 all-reduce.3
where the time goes:
time: 253 us
  waiting for transfers between devices  169 us (67%)
  starting transfers between devices  31.8 us (13%)
  local copies, waits for them, and re-layouts  16 us (6%)
  between operations  13.5 us (5%)
  blocking collectives  12.3 us (5%)
  matrix products  5.34 us (2%)
  other arithmetic  4.23 us (2%)
    all_gather x1, waiting for transfers between devices, local(): lax.all_gather(packed, 'win', axis=0, tiled=True)  98.8 us
    psum x1, waiting for transfers between devices, local(): lax.psum(partial_value.astype(jnp.bfloat16), 'mp').astype(jnp.float32)  37.9 us
    all_to_all x1, waiting for transfers between devices, local(): lax.all_to_all(entry_rows.astype(jnp.bfloat16), ('segment', 'win'), split...  28.3 us
    all_to_all x1, starting transfers between devices, local(): lax.all_to_all(entry_rows.astype(jnp.bfloat16), ('segment', 'win'), split...  16.4 us
    all_to_all x1, starting transfers between devices, local(): lax.all_to_all(gene_slots.astype(jnp.bfloat16), ('segment', 'win'), split...  14 us
    all_gather x1, blocking collectives, local(): all_chan = lax.all_gather(handed, 'mp', axis=0, tiled=True)  12.3 us
    another operation x3, local copies, waits for them, and re-layouts  9.81 us
  transfers between devices with their start and end apart: 5, of which 4 were waited for; matrix products, arithmetic and copies ran while one was open for 1% of the time, Pallas kernels for 0%

commit v1 on v0

v1 whole, which is shorter than its diff:
```python
import math

import jax
import jax.numpy as jnp
from jax import lax
from jax.experimental import pallas as pl
from jax.experimental.pallas import tpu as pltpu
from jax.sharding import PartitionSpec as P

MESH = pl.DeviceIdType.MESH
F32 = jnp.float32
BF16 = jnp.bfloat16

KEY = 64
VAL = 192
TAPS = 5
STEP = 4
BINS = 256
D = 1536
ROWS = 48
COLS = 192
HALF = COLS // 2
P1 = 1024
P2 = 768
TRK = 512
NZ = 8
NY = 4

FORWARD = {
    ("O", 0): ("zp", "zm", "xp", "cp"),
    ("O", -1): ("zp", "cp"),
    ("O", -2): ("zp", "xp", "cp"),
    ("O", -3): ("zp", "xp", "cp"),
    ("O", -4): ("xp", "cp"),
    ("O", 1): ("zm", "cp"),
    ("O", 2): ("zm", "cp"),
    ("O", 3): ("xp", "cp"),
    ("X", 0): ("zp", "zm", "cp"),
    ("X", -1): ("cp",),
    ("X", 1): ("zm", "cp"),
    ("X", 2): ("cp",),
    ("X", -2): ("cp",),
    ("X", -3): ("cp",),
    ("X", 3): ("cp",),
    ("X", -4): ("cp",),
}
ROUNDS = (
    (("O", 0),),
    (("O", -1), ("O", 1), ("X", 0)),
    (("O", -2), ("O", 2), ("X", -1), ("X", 1)),
    (("O", -3), ("O", 3), ("X", -2), ("X", 2)),
    (("O", -4), ("X", -3), ("X", 3)),
    (("X", -4),),
)
SHARDS = tuple(code for group in ROUNDS for code in group)


def nt(left, right):
    return lax.dot_general(left, right, (((1,), (1,)), ((), ())), preferred_element_type=F32)


def nn(left, right):
    return lax.dot_general(left, right, (((1,), (0,)), ((), ())), preferred_element_type=F32)


def tn(left, right):
    return lax.dot_general(left, right, (((0,), (0,)), ((), ())), preferred_element_type=F32)


def gelu(x):
    return 0.5 * x * (1.0 + jnp.tanh(math.sqrt(2.0 / math.pi) * (x + 0.044715 * (x * x * x))))


def kernel(
    feats, p1, p2, outw, cbias, hbias, exon,
    out,
    w1, w2, wo, gx, ga, gr, ft, y, wqt, w2t, trk, gmat, ex_out, ex_in, gs, gin,
    rs1, ss1, rs2, ss2, rsw, ssw, rsy, ssy, rsa, ssa, rsg, ssg, rse, sse, lsem,
):
    s = lax.axis_index("segment")
    w = lax.axis_index("win")
    m = lax.axis_index("mp")
    h = w // (2 * NZ)
    z = (w // 2) % NZ
    c = w % 2
    b = (s + h) % 2
    q = 2 * m + b

    def win_of(hh, zz, cc):
        return hh * (2 * NZ) + zz * 2 + cc

    where = {
        "zp": {"win": win_of(h, (z + 1) % NZ, c)},
        "zm": {"win": win_of(h, (z + NZ - 1) % NZ, c)},
        "xp": {"segment": 1 - s, "win": win_of(1 - h, z, c)},
        "cp": {"win": win_of(h, z, 1 - c)},
        "sp": {"segment": 1 - s},
        "yp": {"mp": (m + 1) % NY},
        "ym": {"mp": (m + NY - 1) % NY},
        "y2": {"mp": (m + 2) % NY},
    }

    def to(name):
        d = {"segment": s, "win": w, "mp": m}
        d.update(where[name])
        return (d["segment"], d["win"], d["mp"])

    barrier = pltpu.get_barrier_semaphore()
    for name in where:
        pl.semaphore_signal(barrier, inc=1, device_id=to(name), device_id_type=MESH)
    pl.semaphore_wait(barrier, len(where))

    def remote(src, dst, send, recv, device):
        return pltpu.make_async_remote_copy(
            src_ref=src, dst_ref=dst, send_sem=send, recv_sem=recv, device_id=device, device_id_type=MESH
        )

    sent = []

    def shard_win(code, core):
        kind, d = code
        return win_of(h if kind == "O" else 1 - h, (z + d + NZ) % NZ, core)

    def ring(own, buf, send, recv):
        count = [0]
        tail = []

        def rows(win):
            return buf.at[pl.ds(pl.multiple_of(win * ROWS, ROWS), ROWS), :]

        def step(r):
            for code in ROUNDS[r]:
                win = shard_win(code, c)
                src = own if code == ("O", 0) else rows(win)
                if code != ("O", 0):
                    remote(src, rows(win), send.at[0], recv.at[win], to("cp")).wait_recv()
                for name in FORWARD[code]:
                    copy = remote(src, rows(win), send.at[count[0]], recv.at[win], to(name))
                    count[0] += 1
                    copy.start()
                    tail.append(copy)

        def rest():
            for code in SHARDS:
                win = shard_win(code, 1 - c)
                remote(rows(win), rows(win), send.at[0], recv.at[win], to("cp")).wait_recv()

        def flush():
            for copy in tail:
                copy.wait_send()

        return step, rest, flush

    def wo_rows(win):
        return wo.at[pl.ds(pl.multiple_of((win % 4) * ROWS, ROWS), ROWS), :]

    def wo_part(win, model):
        return wo.at[
            pl.ds(pl.multiple_of((win % 4) * ROWS, ROWS), ROWS),
            pl.ds(pl.multiple_of(model * 2 * COLS, 2 * COLS), 2 * COLS),
        ]

    home = (w // 4) // 2
    mine = (w // 4) % 2 == b
    wo_hop = (home - m + NY) % NY
    wo_send = jnp.logical_and(mine, wo_hop != 0)
    wo_keep = jnp.logical_and(mine, wo_hop == 0)

    def wo_hop_copy():
        return remote(outw, wo_part(w, m), ssy.at[0], rsy.at[wo_hop], (s, w, home))

    def wo_start():
        @pl.when(wo_send)
        def _():
            wo_hop_copy().start()

        @pl.when(wo_keep)
        def _():
            pltpu.make_async_copy(outw, wo_part(w, m), lsem.at[2]).start()

    wo_count = [0]
    wo_tail = []

    def wo_step(r):
        for code in ROUNDS[r]:
            win = shard_win(code, c)
            first = wo_count[0]
            wo_count[0] += len(FORWARD[code])

            def copies(win=win, code=code, first=first):
                return [
                    remote(wo_rows(win), wo_rows(win), ssw.at[first + i], rsw.at[win % 4], to(name))
                    for i, name in enumerate(FORWARD[code])
                ]

            pred = win // 4 == q
            wo_tail.append((pred, copies))

            @pl.when(pred)
            def _(win=win, code=code, copies=copies):
                if code == ("O", 0):
                    pltpu.make_async_copy(outw, wo_part(w, m), lsem.at[2]).wait()
                    for j in range(1, NY):
                        part = wo_part(w, (m - j + NY) % NY)
                        remote(outw, part, ssy.at[0], rsy.at[j], to("cp")).wait_recv()
                else:
                    remote(wo_rows(win), wo_rows(win), ssw.at[0], rsw.at[win % 4], to("cp")).wait_recv()
                for copy in copies():
                    copy.start()

    def wo_rest():
        for code in SHARDS:
            win = shard_win(code, 1 - c)

            @pl.when(win // 4 == q)
            def _(win=win):
                remote(wo_rows(win), wo_rows(win), ssw.at[0], rsw.at[win % 4], to("cp")).wait_recv()

    def wo_flush():
        @pl.when(wo_send)
        def _():
            wo_hop_copy().wait_send()

        for pred, copies in wo_tail:
            @pl.when(pred)
            def _(copies=copies):
                for copy in copies():
                    copy.wait_send()

    def gather(buf, which):
        def slot(dm, other):
            bb = 1 - b if other else b
            return 2 * ((m + dm + NY) % NY) + bb

        def rows(dm, other, lo=0, n=COLS):
            return buf.at[pl.ds(pl.multiple_of(slot(dm, other) * COLS + lo, 32), n), :]

        def sem(i):
            return rsa.at[which * 9 + i]

        tail = []

        def push(i, r, ref, name):
            copy = remote(ref, ref, ssa.at[which * 9 + i], sem(r), to(name))
            copy.start()
            tail.append(copy)

        def got(r, ref):
            remote(ref, ref, ssa.at[which * 9], sem(r), to("sp")).wait_recv()

        def start():
            own = rows(0, False)
            push(0, 0, own, "yp")
            push(1, 1, own, "ym")
            push(2, 2, own, "sp")

        def first():
            got(0, rows(-1, False))
            push(3, 3, rows(-1, False, 0, HALF), "yp")
            got(1, rows(1, False))
            push(4, 4, rows(1, False, HALF, HALF), "ym")
            got(2, rows(0, True))
            push(5, 5, rows(0, True), "yp")
            push(6, 6, rows(0, True), "ym")

        def second():
            got(3, rows(2, False, 0, HALF))
            got(4, rows(2, False, HALF, HALF))
            push(7, 7, rows(2, False), "sp")

        def third():
            got(5, rows(-1, True))
            got(6, rows(1, True))
            got(7, rows(2, True))

        def flush():
            for copy in tail:
                copy.wait_send()

        return start, first, second, third, flush

    step1, rest1, flush1 = ring(p1, w1, ss1, rs1)
    step2, rest2, flush2 = ring(p2, w2, ss2, rs2)

    step1(0)
    keep1 = pltpu.make_async_copy(p1, w1.at[pl.ds(pl.multiple_of(w * ROWS, ROWS), ROWS), :], lsem.at[0])
    keep2 = pltpu.make_async_copy(p2, w2.at[pl.ds(pl.multiple_of(w * ROWS, ROWS), ROWS), :], lsem.at[1])
    keep1.start()
    keep2.start()
    wo_start()

    eye = (
        lax.broadcasted_iota(jnp.int32, (BINS, BINS), 0) == lax.broadcasted_iota(jnp.int32, (BINS, BINS), 1)
    ).astype(F32).astype(BF16)

    @pl.loop(0, D // BINS)
    def _(n):
        at = pl.ds(pl.multiple_of(n * BINS, BINS), BINS)
        ft[:, at] = nt(eye, feats[at, :]).astype(BF16)

    step1(1)

    rows_id = lax.broadcasted_iota(jnp.int32, (512, 64), 0)
    owner = (
        ((rows_id // 128) % 2) * 32 + ((rows_id // 64) % 2) * 16 + ((rows_id // 8) % 8) * 2 + rows_id // 256
    )
    repeat = (owner == lax.broadcasted_iota(jnp.int32, (512, 64), 1)).astype(F32).astype(BF16)
    first_bin = nn(repeat, exon[0].astype(F32).astype(BF16))
    end_bin = nn(repeat, exon[1].astype(F32).astype(BF16))
    gene = nn(repeat, exon[2].astype(F32).astype(BF16))
    step1(2)
    for blk in range(8):
        at = slice(blk * 64, blk * 64 + 64)
        bins = lax.broadcasted_iota(jnp.int32, (64, BINS), 1).astype(F32)
        which = (lax.broadcasted_iota(jnp.int32, (64, 1), 0) % 8).astype(F32)
        total = jnp.zeros((64, BINS), F32)
        for j in range(8):
            lo = jnp.where(gene[at, j : j + 1] == which, first_bin[at, j : j + 1], 1024.0)
            inside = jnp.logical_and(bins >= lo, bins < end_bin[at, j : j + 1])
            total = total + jnp.where(inside, 1.0, 0.0)
        gmat[at, :] = total.astype(BF16)
        if blk == 3:
            step1(3)
    step1(4)
    step1(5)
    step2(0)
    keep1.wait()
    rest1()

    @pl.loop(0, P1 // 256)
    def _(n):
        at = pl.ds(pl.multiple_of(n * 256, 256), 256)
        y[:, at] = nn(ft[...], w1[:, at])

    t_row = lax.broadcasted_iota(jnp.int32, (BINS, 128), 0)
    lane = lax.broadcasted_iota(jnp.int32, (1, 128), 1)

    def shifted(x, tap):
        by = (tap - TAPS // 2) * STEP
        if by == 0:
            return x
        moved = pltpu.roll(x, (BINS - by) % BINS, 0)
        ok = jnp.logical_and(t_row + by >= 0, t_row + by < BINS)
        return jnp.where(ok, moved, 0.0)

    wide = shifted(y[:, 0:128], 0)
    for tap in range(1, TAPS):
        wide = wide + shifted(y[:, tap * 128 : tap * 128 + 128], tap)
    pairs = [y[:, 640 + i * 128 : 768 + i * 128] for i in range(3)]
    even = shifted(pairs[0], 0) + shifted(pairs[1], 2) + shifted(pairs[2], 4)
    odd = shifted(pairs[0], 1) + shifted(pairs[1], 3)
    narrow = even + pltpu.roll(odd, 64, 1)
    r0, r1, r2 = cbias[0:1, :], cbias[1:2, :], cbias[2:3, :]
    low = lane < 64
    wide_bias = jnp.where(b == 0, r0, pltpu.roll(jnp.where(low, r2, r1), 64, 1))
    narrow_bias = jnp.where(b == 0, r1, pltpu.roll(r2, 64, 1))
    wide = gelu(wide + wide_bias).T
    narrow = gelu(narrow + narrow_bias).T
    base = pl.multiple_of(q * COLS, COLS)
    gx[pl.ds(base, 128), :] = (feats[pl.ds(base, 128), :].astype(F32) + wide).astype(BF16)
    base2 = pl.multiple_of(q * COLS + 128, 64)
    gx[pl.ds(base2, 64), :] = (feats[pl.ds(base2, 64), :].astype(F32) + narrow[:64]).astype(BF16)

    start_x, first_x, second_x, third_x, flush_x = gather(gx, 0)
    start_a, first_a, second_a, third_a, flush_a = gather(ga, 1)
    start_r, first_r, second_r, third_r, flush_r = gather(gr, 2)

    start_x()
    step2(1)
    wqt[...] = nt(eye[:128, :128], w1[:, 896:1024]).astype(BF16)
    step2(2)
    first_x()
    step2(3)
    second_x()
    step2(4)
    step2(5)
    keep2.wait()
    rest2()
    wo_step(0)

    @pl.loop(0, P2 // 256)
    def _(n):
        at = pl.ds(pl.multiple_of(n * 256, 256), 256)
        w2t[at, :] = nt(eye, w2[:, at]).astype(BF16)

    wo_step(1)
    third_x()

    qq = nn(wqt[...], gx[...])[64:128].astype(BF16)
    kv = nn(w2t[0:256, :], gx[...]).astype(BF16)
    scores = tn(kv[0:64], qq) * (1.0 / math.sqrt(KEY))
    weights = jnp.exp(scores)
    prob = (weights / jnp.sum(weights, axis=0, keepdims=True)).astype(BF16)
    ga[pl.ds(base, COLS), :] = nn(kv[64:256], prob).astype(BF16)

    start_a()
    wo_step(2)
    first_a()
    wo_step(3)
    second_a()
    wo_step(4)
    wo_step(5)
    wo_rest()
    third_a()

    resid = gx[pl.ds(base, COLS), :].astype(F32) + nn(wo[...], ga[...])
    gr[pl.ds(base, COLS), :] = resid.astype(BF16)
    start_r()
    first_r()
    second_r()
    third_r()

    for blk in range(TRK // 256):
        logits = nn(w2t[256 + blk * 256 : 512 + blk * 256, :], gr[...])
        bias = hbias[pl.ds(pl.multiple_of(b * TRK + blk * 256, 256), 256), :]
        logits = logits + bias
        soft = jnp.maximum(logits, 0.0) + jnp.log1p(jnp.exp(-jnp.abs(logits)))
        trk[blk * 256 : blk * 256 + 256, :] = soft.astype(BF16)

    def sums(core):
        rows = gmat[pl.ds(pl.multiple_of(core * 256, 256), 256), :]
        left = nt(rows, trk[0:256, :]).reshape(32, 8, 256)
        right = nt(rows, trk[256:512, :]).reshape(32, 8, 256)
        return jnp.concatenate([left, right], axis=1)

    ex_out[...] = sums(1 - c).astype(BF16)
    swap = remote(ex_out, ex_in, sse.at[0], rse.at[0], to("cp"))
    swap.start()
    own_sums = sums(c)
    swap.wait_recv()
    gs[...] = (own_sums + ex_in[...].astype(F32)).astype(BF16)

    def gene_copy(rel):
        ds, dh, dz = rel // 16, (rel // 8) % 2, rel % 8
        s2, h2, z2 = (s + ds) % 2, (h + dh) % 2, (z + dz) % NZ
        return remote(
            gs.at[s2 * 16 + h2 * 8 + z2],
            gin.at[rel],
            ssg.at[rel],
            rsg.at[rel],
            (s2, win_of(h2, z2, c), m),
        )

    @pl.loop(1, 32)
    def _(rel):
        gene_copy(rel).start()

    gin[0] = gs[s * 16 + h * 8 + z]

    @pl.loop(1, 32)
    def _(rel):
        gene_copy(rel).wait_recv()

    same = gin[0].astype(F32)
    other = gin[8].astype(F32)
    for rel in range(1, 8):
        same = same + gin[rel].astype(F32)
        other = other + gin[8 + rel].astype(F32)
    for rel in range(8):
        other = other + gin[16 + rel].astype(F32)
        same = same + gin[24 + rel].astype(F32)
    for value, at in ((same, b), (other, 1 - b)):
        value = jnp.log1p(value)
        out[:, pl.ds(pl.multiple_of(at * TRK, TRK), 256)] = value[0:8]
        out[:, pl.ds(pl.multiple_of(at * TRK + 256, 256), 256)] = value[8:16]

    flush1()
    flush2()
    wo_flush()
    flush_x()
    flush_a()
    flush_r()
    swap.wait_send()

    @pl.loop(1, 32)
    def _(rel):
        gene_copy(rel).wait_send()


def local(feats, conv_w, conv_bias, qkv_w, out_w, head_w, head_bias, exon_lists):
    s = lax.axis_index("segment")
    w = lax.axis_index("win")
    b = (s + w // (2 * NZ)) % 2
    conv = lax.dynamic_slice(conv_w, (0, 0, b * COLS), (ROWS, TAPS, COLS))
    qkv = lax.dynamic_slice(qkv_w, (0, b * 320), (ROWS, 320))
    head = lax.dynamic_slice(head_w, (0, b * TRK), (ROWS, TRK))
    p1 = jnp.concatenate(
        [conv[:, :, :128].reshape(ROWS, 640), conv[:, :, 128:].reshape(ROWS, 320), qkv[:, :KEY]], axis=1
    )
    p2 = jnp.concatenate([qkv[:, KEY:], head], axis=1)
    vmem = pl.BlockSpec(memory_space=pltpu.VMEM)
    dma = pltpu.SemaphoreType.DMA
    return pl.pallas_call(
        kernel,
        out_shape=jax.ShapeDtypeStruct((8, 1024), F32),
        in_specs=[vmem] * 7,
        out_specs=vmem,
        scratch_shapes=[
            pltpu.VMEM((D, P1), BF16),
            pltpu.VMEM((D, P2), BF16),
            pltpu.VMEM((COLS, D), BF16),
            pltpu.VMEM((D, BINS), BF16),
            pltpu.VMEM((D, BINS), BF16),
            pltpu.VMEM((D, BINS), BF16),
            pltpu.VMEM((BINS, D), BF16),
            pltpu.VMEM((BINS, P1), F32),
            pltpu.VMEM((128, D), BF16),
            pltpu.VMEM((P2, D), BF16),
            pltpu.VMEM((TRK, BINS), BF16),
            pltpu.VMEM((512, BINS), BF16),
            pltpu.VMEM((32, 16, 256), BF16),
            pltpu.VMEM((32, 16, 256), BF16),
            pltpu.VMEM((32, 16, 256), BF16),
            pltpu.VMEM((32, 16, 256), BF16),
            dma((32,)), dma((32,)), dma((32,)), dma((32,)), dma((4,)), dma((32,)), dma((4,)), dma((1,)),
            dma((27,)), dma((27,)), dma((32,)), dma((32,)), dma((1,)), dma((1,)), dma((3,)),
        ],
        compiler_params=pltpu.CompilerParams(collective_id=0, has_side_effects=True, vmem_limit_bytes=48 * 1024 * 1024),
    )(
        feats[0], p1, p2, out_w, conv_bias.reshape(3, 128), head_bias.reshape(1024, 1), exon_lists[:, 0],
    )


def solution(mesh):
    in_specs = (
        P("win", None, None),
        P("win", None, "mp"),
        P("mp"),
        P("win", "mp"),
        P("win", "mp"),
        P("win", "mp"),
        P("mp"),
        P(None, "win", None, None),
    )
    return jax.shard_map(
        local, mesh=mesh, in_specs=in_specs, out_specs=P(("segment", "win"), "mp"), check_vma=False
    )
```

time: 253 us -> 103 us (0.41)
  waiting for transfers between devices: 169 us -> 0 us
  Pallas kernels: 0 us -> 98.5 us
  starting transfers between devices: 31.8 us -> 0 us
  between operations: 13.5 us -> 0.15 us
  blocking collectives: 12.3 us -> 0 us
  local copies, waits for them, and re-layouts: 16 us -> 4.02 us
  matrix products: 5.34 us -> 0 us
  other arithmetic: 4.23 us -> 0.09 us
    all_gather x1 -> x0, waiting for transfers between devices: 98.8 us -> none  [local(): lax.all_gather(packed, 'win', axis=0, tiled=True)]
    pallas_call x0 -> x1, Pallas kernels: none -> 98.5 us  [local(): pl.pallas_call(kernel, out_shape=jax.ShapeDtypeStruct((8, 1024), F32), in...]
    psum x1 -> x0, waiting for transfers between devices: 37.9 us -> none  [local(): lax.psum(partial_value.astype(jnp.bfloat16), 'mp').astype(jnp.float32)]
    all_to_all x2 -> x0, starting transfers between devices: 30.4 us -> none  [the longest x1 16.4 us: local(): lax.all_to_all(entry_rows.astype(jnp.bfloat16), ('segment', 'win'), split...]
    all_to_all x2 -> x0, waiting for transfers between devices: 28.3 us -> none  [the longest x1 28.3 us: local(): lax.all_to_all(entry_rows.astype(jnp.bfloat16), ('segment', 'win'), split...]
    all_gather x1 -> x0, blocking collectives: 12.3 us -> none  [local(): all_chan = lax.all_gather(handed, 'mp', axis=0, tiled=True)]
    another operation x3 -> x0, local copies, waits for them, and re-layouts: 9.81 us -> none
    dot_general x6 -> x0, matrix products: 5.34 us -> none  [the longest x5 4.31 us: contract_rows(): lax.dot_general(left, right, (((0,), (0,)), ((), ())), preferred_element_...]
  transfers between devices with their start and end apart: 5 -> 0, of which waited for: 4 -> 0; matrix products, arithmetic and copies ran while one was open for 1% -> 0% of each run, Pallas kernels for 0% -> 0%
where the time goes in v1:
time: 103 us
  Pallas kernels  98.5 us (96%)
  local copies, waits for them, and re-layouts  4.02 us (4%)
    pallas_call x1, Pallas kernels, local(): pl.pallas_call(kernel, out_shape=jax.ShapeDtypeStruct((8, 1024), F32), in...  98.5 us
    unnamed x18, local copies, waits for them, and re-layouts  3.27 us

profile of v1, /device:TPU:1, one launch (start us, length us, event | category | flops | bytes accessed | tf_op | source)
XLA Modules:
  0.0 102.7 jit_solution(12691719287290280729)
XLA Ops:
  0.0 0.0 copy-start
  0.0 0.0 copy-start.5
  0.0 0.0 copy-start.4
  0.1 0.8 copy-done.5
  0.9 0.1 constant_dynamic-slice_fusion
  0.9 0.1 constant_dynamic-slice_fusion.2
  1.0 0.0 copy-done.4
  1.1 0.0 copy-start.1
  1.1 0.0 copy-done
  1.1 0.1 copy_bitcast_fusion
  1.2 0.1 constant_dynamic-slice_fusion.3
  1.3 0.1 reshape.13
  1.5 0.0 copy-start.6
  1.5 0.1 pad_maximum_fusion.p1
  1.6 0.6 copy-done.6
  2.2 0.0 copy-start.7
  2.2 0.1 copy.14
  2.3 0.6 copy-done.7
  2.9 0.0 copy-start.2
  2.9 0.0 copy-start.3
  2.9 0.2 copy.15.hbias
  3.1 0.0 copy-done.1
  3.1 0.5 copy-done.2
  3.6 0.0 copy-done.3
  3.6 98.5 %shard_map.82 = f32[8,1024]{1,0:T(8,128)S(1)} custom-call(bf16[1536,256]{1,0:T(8,128)(2,1)S(1)} %bitcast.9, bf16[48,1024]{1,0:T(8,128)(2,1)S(1)} %pad_maximum_fusion.p1, bf16[48,768]{1,0:T(8,128)(2,1)S(1)} %pad_maximum_fusion.1.p2, bf16[48,384]{1,0:T(8,128)(2,1)S(1)} %copy-done.2, f32[3,128]{1,0:T(4,128)S(1)} %bitcast.11, f32[1024,1]{1,0:T(8,128)S(1)} %copy.15.hbias, ...), custom_call_target="tpu_custom_call" | custom-call | tf_op jit(solution)/shard_map/pallas_call | solution.py:493
  102.1 0.6 copy.19
  (3 shorter events, 0.0 us)
Async XLA Ops:
  0.0 1.1 %copy-start = (bf16[48,5,384]{2,0,1:T(8,128)(2,1)S(1)}, bf16[48,5,384]{2,0,1:T(8,128)(2,1)}, u32[]{:S(2)}) copy-start(bf16[48,5,384]{2,0,1:T(8,128)(2,1)} %param.9) | copy-start | bytes 552964
  0.0 0.9 copy-start.5
  0.0 1.0 %copy-start.4 = (bf16[48,1024]{1,0:T(8,128)(2,1)S(1)}, bf16[48,1024]{1,0:T(8,128)(2,1)}, u32[]{:S(2)}) copy-start(bf16[48,1024]{1,0:T(8,128)(2,1)} %param.13) | copy-start | bytes 294916
  1.1 2.0 %copy-start.1 = (bf16[1,1536,256]{2,1,0:T(8,128)(2,1)S(1)}, bf16[1,1536,256]{2,1,0:T(8,128)(2,1)}, u32[]{:S(2)}) copy-start(bf16[1,1536,256]{2,1,0:T(8,128)(2,1)} %param.8) | copy-start | bytes 2359300
  1.5 0.7 copy-start.6
  2.2 0.7 copy-start.7
  2.9 0.8 copy-start.2
  2.9 0.8 copy-start.3

commit v2 on v1

v2 whole, which is shorter than its diff:
```python
import math

import jax
import jax.numpy as jnp
from jax import lax
from jax.experimental import pallas as pl
from jax.experimental.pallas import tpu as pltpu
from jax.sharding import PartitionSpec as P

MESH = pl.DeviceIdType.MESH
F32 = jnp.float32
BF16 = jnp.bfloat16

KEY = 64
VAL = 192
TAPS = 5
STEP = 4
BINS = 256
D = 1536
ROWS = 48
COLS = 192
WIDE = 640
TAIL = 384
KV = 256
TRK = 512
NZ = 8
NY = 4

QUICK = (
    ((("O", 0), ("zp", "zm", "xp", "zp2", "zm2", "cp")),),
    (
        (("O", -1), ("cp",)),
        (("O", 1), ("cp",)),
        (("X", 0), ("zp", "zm", "cp")),
        (("O", -2), ("zp", "xp", "cp")),
        (("O", 2), ("zm", "cp")),
    ),
    (
        (("O", -3), ("zp", "xp", "cp")),
        (("O", 3), ("xp", "cp")),
        (("X", 1), ("zm", "cp")),
        (("X", -1), ("cp",)),
        (("X", -2), ("cp",)),
    ),
    (
        (("O", -4), ("xp", "cp")),
        (("X", 2), ("cp",)),
        (("X", 3), ("cp",)),
        (("X", -3), ("cp",)),
    ),
    ((("X", -4), ("cp",)),),
)
LEAN = (
    ((("O", 0), ("zp", "zm", "xp", "cp")),),
    ((("O", -1), ("zp", "cp")), (("O", 1), ("zm", "cp")), (("X", 0), ("zp", "zm", "cp"))),
    (
        (("O", -2), ("zp", "xp", "cp")),
        (("O", 2), ("zm", "cp")),
        (("X", 1), ("zm", "cp")),
        (("X", -1), ("cp",)),
    ),
    (
        (("O", -3), ("zp", "xp", "cp")),
        (("O", 3), ("xp", "cp")),
        (("X", 2), ("cp",)),
        (("X", -2), ("cp",)),
    ),
    ((("O", -4), ("xp", "cp")), (("X", 3), ("cp",)), (("X", -3), ("cp",))),
    ((("X", -4), ("cp",)),),
)


def nt(left, right):
    return lax.dot_general(left, right, (((1,), (1,)), ((), ())), preferred_element_type=F32)


def nn(left, right):
    return lax.dot_general(left, right, (((1,), (0,)), ((), ())), preferred_element_type=F32)


def tn(left, right):
    return lax.dot_general(left, right, (((0,), (0,)), ((), ())), preferred_element_type=F32)


def gelu(x):
    return 0.5 * x * (1.0 + jnp.tanh(math.sqrt(2.0 / math.pi) * (x + 0.044715 * (x * x * x))))


def kernel(
    feats_h, conv_h, qkv_h, outw_h, head_h, cbias_h, hbias_h, exon_h,
    out,
    feats, conv, qkv, cbias, hbias, exon, pa, pb, pk, ph, po,
    wa, wb, wk, wh, wo, gx, ga, gr, ft, y, wqt, wkt, wht, hcol, trk, gmat, ex_out, ex_in, gs, gin,
    ring_r, ring_s, rsy, ssy, rsa, ssa, rsg, ssg, rse, sse, lsem,
):
    s = lax.axis_index("segment")
    w = lax.axis_index("win")
    m = lax.axis_index("mp")
    h = w // (2 * NZ)
    z = (w // 2) % NZ
    c = w % 2
    b = (s + h) % 2
    q = 2 * m + b

    def win_of(hh, zz, cc):
        return hh * (2 * NZ) + zz * 2 + cc

    where = {
        "zp": {"win": win_of(h, (z + 1) % NZ, c)},
        "zm": {"win": win_of(h, (z + NZ - 1) % NZ, c)},
        "zp2": {"win": win_of(h, (z + 2) % NZ, c)},
        "zm2": {"win": win_of(h, (z + NZ - 2) % NZ, c)},
        "xp": {"segment": 1 - s, "win": win_of(1 - h, z, c)},
        "cp": {"win": win_of(h, z, 1 - c)},
        "sp": {"segment": 1 - s},
        "yp": {"mp": (m + 1) % NY},
        "ym": {"mp": (m + NY - 1) % NY},
        "y2": {"mp": (m + 2) % NY},
    }

    def to(name):
        d = {"segment": s, "win": w, "mp": m}
        d.update(where[name])
        return (d["segment"], d["win"], d["mp"])

    barrier = pltpu.get_barrier_semaphore()
    for name in where:
        pl.semaphore_signal(barrier, inc=1, device_id=to(name), device_id_type=MESH)

    local_copies = [
        pltpu.make_async_copy(src, dst, lsem.at[i])
        for i, (src, dst) in enumerate(
            (
                (conv_h, conv),
                (qkv_h, qkv),
                (feats_h, feats),
                (head_h.at[:, pl.ds(pl.multiple_of(b * TRK, TRK), TRK)], ph),
                (outw_h, po),
                (exon_h, exon),
                (cbias_h, cbias),
                (hbias_h, hbias),
            )
        )
    ]
    for copy in local_copies:
        copy.start()

    def remote(src, dst, send, recv, device):
        return pltpu.make_async_remote_copy(
            src_ref=src, dst_ref=dst, send_sem=send, recv_sem=recv, device_id=device, device_id_type=MESH
        )

    lane = lax.broadcasted_iota(jnp.int32, (1, 128), 1)
    low = lane < 64
    local_copies[0].wait()
    local_copies[1].wait()
    thin = []
    for tap in range(TAPS):
        part = conv[tap].astype(F32)
        part = jnp.where(b == 0, part, pltpu.roll(part, COLS, 1))
        pa[:, tap * 128 : tap * 128 + 128] = part[:, :128].astype(BF16)
        thin.append(part[:, 128:256])
    head_part = qkv[...].astype(F32)
    head_part = jnp.where(b == 0, head_part, pltpu.roll(head_part, 320, 1))
    thin.append(head_part[:, :128])
    for i in range(3):
        pb[:, i * 128 : i * 128 + 128] = jnp.where(low, thin[2 * i], pltpu.roll(thin[2 * i + 1], 64, 1)).astype(BF16)
    pk[...] = pltpu.roll(head_part, 576, 1)[:, :KV].astype(BF16)

    pl.semaphore_wait(barrier, len(where))

    def ring(index, plan, own, buf):
        count = [0]
        tail = []

        def rows(win):
            return buf.at[pl.ds(pl.multiple_of(win * ROWS, ROWS), ROWS), :]

        def shard_win(code, core):
            kind, d = code
            return win_of(h if kind == "O" else 1 - h, (z + d + NZ) % NZ, core)

        def recv(win):
            return ring_r.at[index, win]

        def wait(win):
            remote(rows(win), rows(win), ring_s.at[index, 0], recv(win), to("cp")).wait_recv()

        def step(r):
            for code, names in plan[r]:
                win = shard_win(code, c)
                src = rows(win)
                if code == ("O", 0):
                    src = rows(win) if own is None else own
                else:
                    wait(win)
                for name in names:
                    copy = remote(src, rows(win), ring_s.at[index, count[0]], recv(win), to(name))
                    count[0] += 1
                    copy.start()
                    tail.append(copy)

        def rest():
            for group in plan:
                for code, names in group:
                    wait(shard_win(code, 1 - c))

        def flush():
            for copy in tail:
                copy.wait_send()

        keep = None
        if own is not None:
            keep = pltpu.make_async_copy(own, rows(w), lsem.at[8 + index])
        return step, rest, flush, keep

    def gather(buf, index, lo, n):
        def rows(dm, other, skip=0, count=n):
            slot = 2 * ((m + dm + NY) % NY) + (1 - b if other else b)
            return buf.at[pl.ds(pl.multiple_of(slot * COLS + lo + skip, 16), count), :]

        half = n // 2
        tail = []

        def push(i, ref, name):
            copy = remote(ref, ref, ssa.at[index, i], rsa.at[index, i], to(name))
            copy.start()
            tail.append(copy)

        def got(i, ref):
            remote(ref, ref, ssa.at[index, i], rsa.at[index, i], to("sp")).wait_recv()

        def start():
            own = rows(0, False)
            push(0, own, "yp")
            push(1, own, "ym")
            push(2, own, "sp")

        def first():
            got(0, rows(-1, False))
            push(3, rows(-1, False, 0, half), "yp")
            got(1, rows(1, False))
            push(4, rows(1, False, half, half), "ym")
            got(2, rows(0, True))
            push(5, rows(0, True), "yp")
            push(6, rows(0, True), "ym")

        def second():
            got(3, rows(2, False, 0, half))
            got(4, rows(2, False, half, half))
            push(7, rows(2, False), "sp")

        def third():
            got(5, rows(-1, True))
            got(6, rows(1, True))
            got(7, rows(2, True))

        def flush():
            for copy in tail:
                copy.wait_send()

        return start, first, second, third, flush

    step_a, rest_a, flush_a, keep_a = ring(0, QUICK, pa, wa)
    step_b, rest_b, flush_b, keep_b = ring(1, QUICK, pb, wb)
    step_k, rest_k, flush_k, keep_k = ring(2, QUICK, pk, wk)
    step_h, rest_h, flush_h, keep_h = ring(3, LEAN, ph, wh)
    step_o, rest_o, flush_o, _ = ring(4, LEAN, None, wo)

    step_a(0)
    step_b(0)
    step_k(0)
    keep_a.start()
    keep_b.start()
    keep_k.start()

    def wo_part(model):
        return wo.at[
            pl.ds(pl.multiple_of(w * ROWS, ROWS), ROWS),
            pl.ds(pl.multiple_of(model * 2 * COLS, 2 * COLS), 2 * COLS),
        ]

    for i in range(2, len(local_copies)):
        local_copies[i].wait()
    keep_h.start()
    keep_o = pltpu.make_async_copy(po, wo_part(m), lsem.at[12])
    keep_o.start()
    hops = (("yp", 1), ("ym", 3), ("y2", 2))
    wo_sends = [remote(po, wo_part(m), ssy.at[j], rsy.at[j], to(name)) for name, j in hops]
    for copy in wo_sends:
        copy.start()

    eye = (
        lax.broadcasted_iota(jnp.int32, (BINS, BINS), 0) == lax.broadcasted_iota(jnp.int32, (BINS, BINS), 1)
    ).astype(F32).astype(BF16)

    @pl.loop(0, D // BINS)
    def _(n):
        at = pl.ds(pl.multiple_of(n * BINS, BINS), BINS)
        ft[:, at] = nt(eye, feats[at, :]).astype(BF16)

    step_a(1)
    step_b(1)
    step_k(1)

    rows_id = lax.broadcasted_iota(jnp.int32, (512, 64), 0)
    owner = (
        ((rows_id // 128) % 2) * 32 + ((rows_id // 64) % 2) * 16 + ((rows_id // 8) % 8) * 2 + rows_id // 256
    )
    repeat = (owner == lax.broadcasted_iota(jnp.int32, (512, 64), 1)).astype(F32).astype(BF16)
    first_bin = nt(repeat, exon[0].astype(F32).astype(BF16))
    end_bin = nt(repeat, exon[1].astype(F32).astype(BF16))
    gene = nt(repeat, exon[2].astype(F32).astype(BF16))

    def gene_bins(blk):
        at = slice(blk * 64, blk * 64 + 64)
        bins = lax.broadcasted_iota(jnp.int32, (64, BINS), 1).astype(F32)
        which = (lax.broadcasted_iota(jnp.int32, (64, 1), 0) % 8).astype(F32)
        total = jnp.zeros((64, BINS), F32)
        for j in range(8):
            lo = jnp.where(gene[at, j : j + 1] == which, first_bin[at, j : j + 1], 1024.0)
            inside = jnp.logical_and(bins >= lo, bins < end_bin[at, j : j + 1])
            total = total + jnp.where(inside, 1.0, 0.0)
        gmat[at, :] = total.astype(BF16)

    for blk in range(2):
        gene_bins(blk)
    step_a(2)
    step_b(2)
    step_k(2)
    for blk in range(2, 4):
        gene_bins(blk)
    step_a(3)
    step_b(3)
    step_k(3)
    keep_o.wait()
    for name, j in hops:
        remote(po, wo_part((m - j + NY) % NY), ssy.at[j], rsy.at[j], to("cp")).wait_recv()
    step_h(0)
    step_o(0)
    step_a(4)
    step_b(4)
    keep_a.wait()
    rest_a()

    t_row = lax.broadcasted_iota(jnp.int32, (BINS, 128), 0)

    def shifted(x, tap):
        by = (tap - TAPS // 2) * STEP
        if by == 0:
            return x
        moved = pltpu.roll(x, (BINS - by) % BINS, 0)
        ok = jnp.logical_and(t_row + by >= 0, t_row + by < BINS)
        return jnp.where(ok, moved, 0.0)

    start_x, first_x, second_x, third_x, flush_x = gather(gx, 0, 0, 128)
    start_u, first_u, second_u, third_u, flush_u = gather(gx, 1, 128, 64)
    start_v, first_v, second_v, third_v, flush_v = gather(ga, 2, 0, 96)
    start_w, first_w, second_w, third_w, flush_w = gather(ga, 3, 96, 96)

    c0, c1, c2 = (cbias[i * 128 : i * 128 + 128].reshape(1, 128) for i in range(3))
    wide_bias = jnp.where(b == 0, c0, pltpu.roll(jnp.where(low, c2, c1), 64, 1))
    narrow_bias = jnp.where(b == 0, c1, pltpu.roll(c2, 64, 1))
    base = pl.multiple_of(q * COLS, COLS)
    base2 = pl.multiple_of(q * COLS + 128, 64)

    for i in range(TAPS):
        y[:, i * 128 : i * 128 + 128] = nn(ft[...], wa[:, i * 128 : i * 128 + 128])
    wide = shifted(y[:, 0:128], 0)
    for tap in range(1, TAPS):
        wide = wide + shifted(y[:, tap * 128 : tap * 128 + 128], tap)
    wide = gelu(wide + wide_bias).T
    gx[pl.ds(base, 128), :] = (feats[pl.ds(base, 128), :].astype(F32) + wide).astype(BF16)
    start_x()

    keep_b.wait()
    rest_b()
    pairs = [nn(ft[...], wb[:, i * 128 : i * 128 + 128]) for i in range(3)]
    even = shifted(pairs[0], 0) + shifted(pairs[1], 2) + shifted(pairs[2], 4)
    odd = shifted(pairs[0], 1) + shifted(pairs[1], 3)
    narrow = even + pltpu.roll(odd, 64, 1)
    narrow = gelu(narrow + narrow_bias).T
    gx[pl.ds(base2, 64), :] = (feats[pl.ds(base2, 64), :].astype(F32) + narrow[:64]).astype(BF16)
    start_u()

    step_k(4)
    keep_k.wait()
    step_h(1)
    step_o(1)
    first_x()
    first_u()
    step_h(2)
    step_o(2)
    rest_k()
    wqt[...] = nt(eye[:128, :128], wb[:, 256:384]).astype(BF16)
    wkt[...] = nt(eye, wk[...]).astype(BF16)
    second_x()
    second_u()
    step_h(3)
    third_x()
    third_u()

    qq = nn(wqt[...], gx[...])[64:128].astype(BF16)
    kv = nn(wkt[...], gx[...]).astype(BF16)
    scores = tn(kv[0:64], qq) * (1.0 / math.sqrt(KEY))
    weights = jnp.exp(scores)
    prob = (weights / jnp.sum(weights, axis=0, keepdims=True)).astype(BF16)
    ga[pl.ds(base, COLS), :] = nn(kv[64:256], prob).astype(BF16)

    start_v()
    start_w()
    step_o(3)
    step_h(4)
    for blk in range(4, 8):
        gene_bins(blk)
    first_v()
    first_w()
    step_o(4)
    step_h(5)
    keep_h.wait()
    rest_h()
    flush_a()
    flush_b()
    second_v()
    second_w()
    for i in range(TRK // 256):
        wht[i * 256 : i * 256 + 256, :] = nt(eye, wh[:, i * 256 : i * 256 + 256]).astype(BF16)
    eye_f = (
        lax.broadcasted_iota(jnp.int32, (128, 128), 0) == lax.broadcasted_iota(jnp.int32, (128, 128), 1)
    )
    for i in range(TRK // 128):
        row = jnp.where(b == 0, hbias[i : i + 1, :], hbias[4 + i : 5 + i, :])
        hcol[i * 128 : i * 128 + 128, :] = jnp.sum(jnp.where(eye_f, row, 0.0), axis=1, keepdims=True)
    step_o(5)
    third_v()
    third_w()
    rest_o()

    for i in range(D // 256):
        at = slice(i * 256, i * 256 + 256)
        gr[at, :] = (gx[at, :].astype(F32) + nn(wo[at, :], ga[...])).astype(BF16)

    for blk in range(TRK // 256):
        at = slice(blk * 256, blk * 256 + 256)
        logits = nn(wht[at, :], gr[...]) + hcol[at, :]
        soft = jnp.maximum(logits, 0.0) + jnp.log1p(jnp.exp(-jnp.abs(logits)))
        trk[at, :] = soft.astype(BF16)

    def sums(core):
        rows = gmat[pl.ds(pl.multiple_of(core * 256, 256), 256), :]
        left = nt(rows, trk[0:256, :]).reshape(32, 8, 256)
        right = nt(rows, trk[256:512, :]).reshape(32, 8, 256)
        return jnp.concatenate([left, right], axis=1)

    ex_out[...] = sums(1 - c).astype(BF16)
    swap = remote(ex_out, ex_in, sse.at[0], rse.at[0], to("cp"))
    swap.start()
    own_sums = sums(c)
    swap.wait_recv()
    gs[...] = (own_sums + ex_in[...].astype(F32)).astype(BF16)

    def gene_copy(rel):
        ds, dh, dz = rel // 16, (rel // 8) % 2, rel % 8
        s2, h2, z2 = (s + ds) % 2, (h + dh) % 2, (z + dz) % NZ
        return remote(
            gs.at[s2 * 16 + h2 * 8 + z2],
            gin.at[rel],
            ssg.at[rel],
            rsg.at[rel],
            (s2, win_of(h2, z2, c), m),
        )

    @pl.loop(1, 32)
    def _(rel):
        gene_copy(rel).start()

    gin[0] = gs[s * 16 + h * 8 + z]
    flush_k()
    flush_h()
    flush_o()
    flush_x()
    flush_u()
    flush_v()
    flush_w()
    for copy in wo_sends:
        copy.wait_send()
    swap.wait_send()

    @pl.loop(1, 32)
    def _(rel):
        gene_copy(rel).wait()

    same = gin[0].astype(F32)
    other = gin[8].astype(F32)
    for rel in range(1, 8):
        same = same + gin[rel].astype(F32)
        other = other + gin[8 + rel].astype(F32)
    for rel in range(8):
        other = other + gin[16 + rel].astype(F32)
        same = same + gin[24 + rel].astype(F32)
    for value, at in ((same, b), (other, 1 - b)):
        value = jnp.log1p(value)
        out[:, pl.ds(pl.multiple_of(at * TRK, TRK), 256)] = value[0:8]
        out[:, pl.ds(pl.multiple_of(at * TRK + 256, 256), 256)] = value[8:16]


def local(feats, conv_w, conv_bias, qkv_w, out_w, head_w, head_bias, exon_lists):
    vmem = pltpu.VMEM
    dma = pltpu.SemaphoreType.DMA
    anywhere = pl.BlockSpec(memory_space=pltpu.HBM)
    return pl.pallas_call(
        kernel,
        out_shape=jax.ShapeDtypeStruct((8, 1024), F32),
        in_specs=[anywhere] * 8,
        out_specs=pl.BlockSpec(memory_space=pltpu.VMEM),
        scratch_shapes=[
            vmem((D, BINS), BF16),
            vmem((TAPS, ROWS, 2 * COLS), BF16),
            vmem((ROWS, 640), BF16),
            vmem((384,), F32),
            vmem((8, 128), F32),
            vmem((3, 8, 64), jnp.int32),
            vmem((ROWS, WIDE), BF16),
            vmem((ROWS, TAIL), BF16),
            vmem((ROWS, KV), BF16),
            vmem((ROWS, TRK), BF16),
            vmem((ROWS, 2 * COLS), BF16),
            vmem((D, WIDE), BF16),
            vmem((D, TAIL), BF16),
            vmem((D, KV), BF16),
            vmem((D, TRK), BF16),
            vmem((D, D), BF16),
            vmem((D, BINS), BF16),
            vmem((D, BINS), BF16),
            vmem((D, BINS), BF16),
            vmem((BINS, D), BF16),
            vmem((BINS, WIDE), F32),
            vmem((128, D), BF16),
            vmem((KV, D), BF16),
            vmem((TRK, D), BF16),
            vmem((TRK, 1), F32),
            vmem((TRK, BINS), BF16),
            vmem((512, BINS), BF16),
            vmem((32, 16, 256), BF16),
            vmem((32, 16, 256), BF16),
            vmem((32, 16, 256), BF16),
            vmem((32, 16, 256), BF16),
            dma((5, 32)), dma((5, 34)), dma((4,)), dma((4,)),
            dma((4, 8)), dma((4, 8)), dma((32,)), dma((32,)), dma((1,)), dma((1,)), dma((13,)),
        ],
        compiler_params=pltpu.CompilerParams(
            collective_id=0, has_side_effects=True, vmem_limit_bytes=60 * 1024 * 1024
        ),
    )(
        feats[0],
        conv_w.transpose(1, 0, 2),
        qkv_w,
        out_w,
        head_w,
        conv_bias,
        head_bias.reshape(8, 128),
        exon_lists[:, 0].transpose(0, 2, 1),
    )


def solution(mesh):
    in_specs = (
        P("win", None, None),
        P("win", None, "mp"),
        P("mp"),
        P("win", "mp"),
        P("win", "mp"),
        P("win", "mp"),
        P("mp"),
        P(None, "win", None, None),
    )
    return jax.shard_map(
        local, mesh=mesh, in_specs=in_specs, out_specs=P(("segment", "win"), "mp"), check_vma=False
    )
```

time: 103 us -> 84.7 us (0.82)
  Pallas kernels: 98.5 us -> 83.1 us
  local copies, waits for them, and re-layouts: 4.02 us -> 1.38 us
    pallas_call x1, Pallas kernels: 98.5 us -> 83.1 us  [local(): pl.pallas_call(kernel, out_shape=jax.ShapeDtypeStruct((8, 1024), F32), in...]
    unnamed x18 -> x1, local copies, waits for them, and re-layouts: 3.27 us -> 1.38 us
where the time goes in v2:
time: 84.7 us; the launch traced here: 84.5 us
  Pallas kernels  83.1 us (98%)
  local copies, waits for them, and re-layouts  1.38 us (2%)
    pallas_call x1, Pallas kernels, local(): pl.pallas_call(kernel, out_shape=jax.ShapeDtypeStruct((8, 1024), F32), in...  83.1 us

profile of v2, /device:TPU:1, one launch (start us, length us, event | category | flops | bytes accessed | tf_op | source)
XLA Modules:
  0.0 84.5 jit_solution(3183686653266346357)
XLA Ops:
  0.0 83.1 %shard_map.82 = f32[8,1024]{1,0:T(8,128)} custom-call(bf16[1536,256]{1,0:T(8,128)(2,1)} %bitcast.6, bf16[5,48,384]{2,1,0:T(8,128)(2,1)} %bitcast.7, bf16[48,640]{1,0:T(8,128)(2,1)} %qkv_h.1, bf16[48,384]{1,0:T(8,128)(2,1)} %outw_h.1, bf16[48,1024]{1,0:T(8,128)(2,1)} %head_h.1, f32[384]{0:T(512)} %cbias_h.1, f32[8,128]{1,0:T(8,128)} %bitcast.9, ...), custom_call_target="tpu_custom_call" | custom-call | tf_op jit(solution)/shard_map/pallas_call | solution.py:511
  83.1 1.4 %copy.10 = f32[8,1024]{1,0:T(8,128)} copy(f32[8,1024]{1,0:T(8,128)} %shard_map.82) | data formatting | bytes 65536

commit v3 on v2

--- a/solution.py
+++ b/solution.py
@@ -90,7 +90,7 @@
     feats_h, conv_h, qkv_h, outw_h, head_h, cbias_h, hbias_h, exon_h,
     out,
     feats, conv, qkv, cbias, hbias, exon, pa, pb, pk, ph, po,
-    wa, wb, wk, wh, wo, gx, ga, gr, ft, y, wqt, wkt, wht, hcol, trk, gmat, ex_out, ex_in, gs, gin,
+    wa, wb, wk, wh, wo, wo2, gx, ga, gr, ft, y, wqt, wkt, wht, hcol, trk, gmat, ex_out, ex_in, gs, gin,
     ring_r, ring_s, rsy, ssy, rsa, ssa, rsg, ssg, rse, sse, lsem,
 ):
     s = lax.axis_index("segment")
@@ -266,29 +266,44 @@
     step_k, rest_k, flush_k, keep_k = ring(2, QUICK, pk, wk)
     step_h, rest_h, flush_h, keep_h = ring(3, LEAN, ph, wh)
     step_o, rest_o, flush_o, _ = ring(4, LEAN, None, wo)
+    step_p, rest_p, flush_p, _ = ring(5, LEAN, None, wo2)
 
     step_a(0)
     step_b(0)
-    step_k(0)
     keep_a.start()
     keep_b.start()
     keep_k.start()
 
-    def wo_part(model):
-        return wo.at[
+    def wo_part(buf, model):
+        return buf.at[
             pl.ds(pl.multiple_of(w * ROWS, ROWS), ROWS),
-            pl.ds(pl.multiple_of(model * 2 * COLS, 2 * COLS), 2 * COLS),
+            pl.ds(pl.multiple_of((model % 2) * 2 * COLS, 2 * COLS), 2 * COLS),
         ]
 
     for i in range(2, len(local_copies)):
         local_copies[i].wait()
     keep_h.start()
-    keep_o = pltpu.make_async_copy(po, wo_part(m), lsem.at[12])
-    keep_o.start()
+
+    def each_part(model, act):
+        @pl.when(model < 2)
+        def _():
+            act(wo_part(wo, model))
+
+        @pl.when(model >= 2)
+        def _():
+            act(wo_part(wo2, model))
+
     hops = (("yp", 1), ("ym", 3), ("y2", 2))
-    wo_sends = [remote(po, wo_part(m), ssy.at[j], rsy.at[j], to(name)) for name, j in hops]
-    for copy in wo_sends:
-        copy.start()
+    each_part(m, lambda ref: pltpu.make_async_copy(po, ref, lsem.at[12]).start())
+    for name, j in hops:
+        each_part(m, lambda ref, name=name, j=j: remote(po, ref, ssy.at[j], rsy.at[j], to(name)).start())
+
+    def wo_ready():
+        each_part(m, lambda ref: pltpu.make_async_copy(po, ref, lsem.at[12]).wait())
+        for name, j in hops:
+            each_part(
+                (m - j + NY) % NY, lambda ref, j=j: remote(po, ref, ssy.at[j], rsy.at[j], to("cp")).wait_recv()
+            )
 
     eye = (
         lax.broadcasted_iota(jnp.int32, (BINS, BINS), 0) == lax.broadcasted_iota(jnp.int32, (BINS, BINS), 1)
@@ -301,7 +316,7 @@
 
     step_a(1)
     step_b(1)
-    step_k(1)
+    step_k(0)
 
     rows_id = lax.broadcasted_iota(jnp.int32, (512, 64), 0)
     owner = (
@@ -327,19 +342,18 @@
         gene_bins(blk)
     step_a(2)
     step_b(2)
-    step_k(2)
+    step_k(1)
     for blk in range(2, 4):
         gene_bins(blk)
     step_a(3)
     step_b(3)
-    step_k(3)
-    keep_o.wait()
-    for name, j in hops:
-        remote(po, wo_part((m - j + NY) % NY), ssy.at[j], rsy.at[j], to("cp")).wait_recv()
+    step_k(2)
     step_h(0)
-    step_o(0)
     step_a(4)
     step_b(4)
+    wo_ready()
+    step_o(0)
+    step_p(0)
     keep_a.wait()
     rest_a()
 
@@ -383,20 +397,22 @@
     gx[pl.ds(base2, 64), :] = (feats[pl.ds(base2, 64), :].astype(F32) + narrow[:64]).astype(BF16)
     start_u()
 
-    step_k(4)
-    keep_k.wait()
+    step_k(3)
     step_h(1)
     step_o(1)
+    step_p(1)
     first_x()
     first_u()
+    step_k(4)
     step_h(2)
     step_o(2)
-    rest_k()
+    keep_k.wait()
     wqt[...] = nt(eye[:128, :128], wb[:, 256:384]).astype(BF16)
-    wkt[...] = nt(eye, wk[...]).astype(BF16)
     second_x()
     second_u()
-    step_h(3)
+    step_p(2)
+    rest_k()
+    wkt[...] = nt(eye, wk[...]).astype(BF16)
     third_x()
     third_u()
 
@@ -409,20 +425,25 @@
 
     start_v()
     start_w()
+    step_h(3)
     step_o(3)
-    step_h(4)
+    step_p(3)
     for blk in range(4, 8):
         gene_bins(blk)
     first_v()
     first_w()
+    step_h(4)
     step_o(4)
-    step_h(5)
-    keep_h.wait()
-    rest_h()
+    step_p(4)
     flush_a()
     flush_b()
     second_v()
     second_w()
+    step_h(5)
+    step_o(5)
+    step_p(5)
+    keep_h.wait()
+    rest_h()
     for i in range(TRK // 256):
         wht[i * 256 : i * 256 + 256, :] = nt(eye, wh[:, i * 256 : i * 256 + 256]).astype(BF16)
     eye_f = (
@@ -431,33 +452,35 @@
     for i in range(TRK // 128):
         row = jnp.where(b == 0, hbias[i : i + 1, :], hbias[4 + i : 5 + i, :])
         hcol[i * 128 : i * 128 + 128, :] = jnp.sum(jnp.where(eye_f, row, 0.0), axis=1, keepdims=True)
-    step_o(5)
     third_v()
     third_w()
     rest_o()
+    rest_p()
 
     for i in range(D // 256):
         at = slice(i * 256, i * 256 + 256)
-        gr[at, :] = (gx[at, :].astype(F32) + nn(wo[at, :], ga[...])).astype(BF16)
-
+        gr[at, :] = (gx[at, :].astype(F32) + (nn(wo[at, :], ga[0 : D // 2, :]) + nn(wo2[at, :], ga[D // 2 :, :]))).astype(BF16)
+
+    def sums(core, blk):
+        rows = gmat[pl.ds(pl.multiple_of(core * 256, 256), 256), :]
+        return nt(rows, trk[blk * 256 : blk * 256 + 256, :]).reshape(32, 8, 256)
+
+    swaps = []
     for blk in range(TRK // 256):
         at = slice(blk * 256, blk * 256 + 256)
         logits = nn(wht[at, :], gr[...]) + hcol[at, :]
         soft = jnp.maximum(logits, 0.0) + jnp.log1p(jnp.exp(-jnp.abs(logits)))
         trk[at, :] = soft.astype(BF16)
-
-    def sums(core):
-        rows = gmat[pl.ds(pl.multiple_of(core * 256, 256), 256), :]
-        left = nt(rows, trk[0:256, :]).reshape(32, 8, 256)
-        right = nt(rows, trk[256:512, :]).reshape(32, 8, 256)
-        return jnp.concatenate([left, right], axis=1)
-
-    ex_out[...] = sums(1 - c).astype(BF16)
-    swap = remote(ex_out, ex_in, sse.at[0], rse.at[0], to("cp"))
-    swap.start()
-    own_sums = sums(c)
-    swap.wait_recv()
-    gs[...] = (own_sums + ex_in[...].astype(F32)).astype(BF16)
+        give = sums(1 - c, blk)
+        ex_out[blk] = jnp.concatenate([give[:, :, :128], give[:, :, 128:]], axis=1).astype(BF16)
+        swaps.append(remote(ex_out.at[blk], ex_in.at[blk], sse.at[blk], rse.at[blk], to("cp")))
+        swaps[blk].start()
+    keep_sums = [sums(c, blk) for blk in range(TRK // 256)]
+    for blk in range(TRK // 256):
+        swaps[blk].wait_recv()
+        took = ex_in[blk].astype(F32)
+        keep_sums[blk] = keep_sums[blk] + jnp.concatenate([took[:, :8], took[:, 8:]], axis=2)
+    gs[...] = jnp.concatenate(keep_sums, axis=1).astype(BF16)
 
     def gene_copy(rel):
         ds, dh, dz = rel // 16, (rel // 8) % 2, rel % 8
@@ -470,25 +493,25 @@
             (s2, win_of(h2, z2, c), m),
         )
 
-    @pl.loop(1, 32)
-    def _(rel):
-        gene_copy(rel).start()
+    gene_copies = [gene_copy(part * 8 + dz) for dz in (4, 3, 5, 2, 6, 1, 7, 0) for part in (3, 2, 1, 0) if part + dz]
+    for copy in gene_copies:
+        copy.start()
 
     gin[0] = gs[s * 16 + h * 8 + z]
     flush_k()
     flush_h()
     flush_o()
+    flush_p()
     flush_x()
     flush_u()
     flush_v()
     flush_w()
-    for copy in wo_sends:
-        copy.wait_send()
-    swap.wait_send()
-
-    @pl.loop(1, 32)
-    def _(rel):
-        gene_copy(rel).wait()
+    for name, j in hops:
+        each_part(m, lambda ref, name=name, j=j: remote(po, ref, ssy.at[j], rsy.at[j], to(name)).wait_send())
+    for swap in swaps:
+        swap.wait_send()
+    for copy in gene_copies:
+        copy.wait()
 
     same = gin[0].astype(F32)
     other = gin[8].astype(F32)
@@ -529,7 +552,8 @@
             vmem((D, TAIL), BF16),
             vmem((D, KV), BF16),
             vmem((D, TRK), BF16),
-            vmem((D, D), BF16),
+            vmem((D, D // 2), BF16),
+            vmem((D, D // 2), BF16),
             vmem((D, BINS), BF16),
             vmem((D, BINS), BF16),
             vmem((D, BINS), BF16),
@@ -541,12 +565,12 @@
             vmem((TRK, 1), F32),
             vmem((TRK, BINS), BF16),
             vmem((512, BINS), BF16),
+            vmem((2, 32, 16, 128), BF16),
+            vmem((2, 32, 16, 128), BF16),
             vmem((32, 16, 256), BF16),
             vmem((32, 16, 256), BF16),
-            vmem((32, 16, 256), BF16),
-            vmem((32, 16, 256), BF16),
-            dma((5, 32)), dma((5, 34)), dma((4,)), dma((4,)),
-            dma((4, 8)), dma((4, 8)), dma((32,)), dma((32,)), dma((1,)), dma((1,)), dma((13,)),
+            dma((6, 32)), dma((6, 34)), dma((4,)), dma((4,)),
+            dma((4, 8)), dma((4, 8)), dma((32,)), dma((32,)), dma((2,)), dma((2,)), dma((13,)),
         ],
         compiler_params=pltpu.CompilerParams(
             collective_id=0, has_side_effects=True, vmem_limit_bytes=60 * 1024 * 1024

time: 84.7 us -> 81.3 us (0.960)
  Pallas kernels: 83.1 us -> 79.8 us
    pallas_call x1, Pallas kernels: 83.1 us -> 79.8 us  [local(): pl.pallas_call(kernel, out_shape=jax.ShapeDtypeStruct((8, 1024), F32), in...]
where the time goes in v3:
time: 81.3 us; the launch traced here: 81.2 us
  Pallas kernels  79.8 us (98%)
  local copies, waits for them, and re-layouts  1.38 us (2%)
    pallas_call x1, Pallas kernels, local(): pl.pallas_call(kernel, out_shape=jax.ShapeDtypeStruct((8, 1024), F32), in...  79.8 us

profile of v3, /device:TPU:1, one launch (start us, length us, event | category | flops | bytes accessed | tf_op | source)
XLA Modules:
  0.0 81.2 jit_solution(6752242711451221579)
XLA Ops:
  0.0 79.8 %shard_map.82 = f32[8,1024]{1,0:T(8,128)} custom-call(bf16[1536,256]{1,0:T(8,128)(2,1)} %bitcast.6, bf16[5,48,384]{2,1,0:T(8,128)(2,1)} %bitcast.7, bf16[48,640]{1,0:T(8,128)(2,1)} %qkv_h.1, bf16[48,384]{1,0:T(8,128)(2,1)} %outw_h.1, bf16[48,1024]{1,0:T(8,128)(2,1)} %head_h.1, f32[384]{0:T(512)} %cbias_h.1, f32[8,128]{1,0:T(8,128)} %bitcast.9, ...), custom_call_target="tpu_custom_call" | custom-call | tf_op jit(solution)/shard_map/pallas_call | solution.py:534
  79.8 1.4 %copy.10 = f32[8,1024]{1,0:T(8,128)} copy(f32[8,1024]{1,0:T(8,128)} %shard_map.82) | data formatting | bytes 65536

commit v4 on v3

--- a/solution.py
+++ b/solution.py
@@ -263,13 +263,19 @@
 
     step_a, rest_a, flush_a, keep_a = ring(0, QUICK, pa, wa)
     step_b, rest_b, flush_b, keep_b = ring(1, QUICK, pb, wb)
-    step_k, rest_k, flush_k, keep_k = ring(2, QUICK, pk, wk)
+    step_k, rest_k, flush_k, keep_k = ring(2, LEAN, pk, wk)
     step_h, rest_h, flush_h, keep_h = ring(3, LEAN, ph, wh)
     step_o, rest_o, flush_o, _ = ring(4, LEAN, None, wo)
     step_p, rest_p, flush_p, _ = ring(5, LEAN, None, wo2)
 
+    start_x, first_x, second_x, third_x, flush_x = gather(gx, 0, 0, 128)
+    start_u, first_u, second_u, third_u, flush_u = gather(gx, 1, 128, 64)
+    start_v, first_v, second_v, third_v, flush_v = gather(ga, 2, 0, 96)
+    start_w, first_w, second_w, third_w, flush_w = gather(ga, 3, 96, 96)
+
     step_a(0)
     step_b(0)
+    step_k(0)
     keep_a.start()
     keep_b.start()
     keep_k.start()
@@ -316,7 +322,7 @@
 
     step_a(1)
     step_b(1)
-    step_k(0)
+    step_h(0)
 
     rows_id = lax.broadcasted_iota(jnp.int32, (512, 64), 0)
     owner = (
@@ -343,17 +349,16 @@
     step_a(2)
     step_b(2)
     step_k(1)
-    for blk in range(2, 4):
-        gene_bins(blk)
+    step_h(1)
     step_a(3)
     step_b(3)
     step_k(2)
-    step_h(0)
-    step_a(4)
-    step_b(4)
     wo_ready()
     step_o(0)
     step_p(0)
+    step_a(4)
+    step_h(2)
+    step_b(4)
     keep_a.wait()
     rest_a()
 
@@ -366,11 +371,6 @@
         moved = pltpu.roll(x, (BINS - by) % BINS, 0)
         ok = jnp.logical_and(t_row + by >= 0, t_row + by < BINS)
         return jnp.where(ok, moved, 0.0)
-
-    start_x, first_x, second_x, third_x, flush_x = gather(gx, 0, 0, 128)
-    start_u, first_u, second_u, third_u, flush_u = gather(gx, 1, 128, 64)
-    start_v, first_v, second_v, third_v, flush_v = gather(ga, 2, 0, 96)
-    start_w, first_w, second_w, third_w, flush_w = gather(ga, 3, 96, 96)
 
     c0, c1, c2 = (cbias[i * 128 : i * 128 + 128].reshape(1, 128) for i in range(3))
     wide_bias = jnp.where(b == 0, c0, pltpu.roll(jnp.where(low, c2, c1), 64, 1))
@@ -389,6 +389,7 @@
 
     keep_b.wait()
     rest_b()
+    step_o(1)
     pairs = [nn(ft[...], wb[:, i * 128 : i * 128 + 128]) for i in range(3)]
     even = shifted(pairs[0], 0) + shifted(pairs[1], 2) + shifted(pairs[2], 4)
     odd = shifted(pairs[0], 1) + shifted(pairs[1], 3)
@@ -396,25 +397,26 @@
     narrow = gelu(narrow + narrow_bias).T
     gx[pl.ds(base2, 64), :] = (feats[pl.ds(base2, 64), :].astype(F32) + narrow[:64]).astype(BF16)
     start_u()
-
     step_k(3)
-    step_h(1)
-    step_o(1)
     step_p(1)
     first_x()
+    step_h(3)
+    for blk in range(2, 4):
+        gene_bins(blk)
     first_u()
-    step_k(4)
-    step_h(2)
     step_o(2)
-    keep_k.wait()
     wqt[...] = nt(eye[:128, :128], wb[:, 256:384]).astype(BF16)
     second_x()
+    step_k(4)
     second_u()
     step_p(2)
+    third_x()
+    step_k(5)
+    step_o(3)
+    third_u()
+    keep_k.wait()
     rest_k()
     wkt[...] = nt(eye, wk[...]).astype(BF16)
-    third_x()
-    third_u()
 
     qq = nn(wqt[...], gx[...])[64:128].astype(BF16)
     kv = nn(wkt[...], gx[...]).astype(BF16)
@@ -424,26 +426,23 @@
     ga[pl.ds(base, COLS), :] = nn(kv[64:256], prob).astype(BF16)
 
     start_v()
+    step_h(4)
+    step_p(3)
     start_w()
-    step_h(3)
-    step_o(3)
-    step_p(3)
-    for blk in range(4, 8):
+    for blk in range(4, 6):
         gene_bins(blk)
     first_v()
+    step_h(5)
+    step_o(4)
     first_w()
-    step_h(4)
-    step_o(4)
-    step_p(4)
-    flush_a()
-    flush_b()
-    second_v()
-    second_w()
-    step_h(5)
-    step_o(5)
-    step_p(5)
     keep_h.wait()
     rest_h()
+    step_p(4)
+    for blk in range(6, 8):
+        gene_bins(blk)
+    second_v()
+    step_o(5)
+    second_w()
     for i in range(TRK // 256):
         wht[i * 256 : i * 256 + 256, :] = nt(eye, wh[:, i * 256 : i * 256 + 256]).astype(BF16)
     eye_f = (
@@ -452,6 +451,9 @@
     for i in range(TRK // 128):
         row = jnp.where(b == 0, hbias[i : i + 1, :], hbias[4 + i : 5 + i, :])
         hcol[i * 128 : i * 128 + 128, :] = jnp.sum(jnp.where(eye_f, row, 0.0), axis=1, keepdims=True)
+    step_p(5)
+    flush_a()
+    flush_b()
     third_v()
     third_w()
     rest_o()

time: 81.3 us -> 79.4 us (0.977)
  Pallas kernels: 79.8 us -> 77.8 us
    pallas_call x1, Pallas kernels: 79.8 us -> 77.8 us  [local(): pl.pallas_call(kernel, out_shape=jax.ShapeDtypeStruct((8, 1024), F32), in...]
where the time goes in v4:
time: 79.4 us; the launch traced here: 79.2 us
  Pallas kernels  77.8 us (98%)
  local copies, waits for them, and re-layouts  1.38 us (2%)
    pallas_call x1, Pallas kernels, local(): pl.pallas_call(kernel, out_shape=jax.ShapeDtypeStruct((8, 1024), F32), in...  77.8 us

profile of v4, /device:TPU:1, one launch (start us, length us, event | category | flops | bytes accessed | tf_op | source)
XLA Modules:
  0.0 79.2 jit_solution(3928692985497131892)
XLA Ops:
  0.0 77.8 %shard_map.82 = f32[8,1024]{1,0:T(8,128)} custom-call(bf16[1536,256]{1,0:T(8,128)(2,1)} %bitcast.6, bf16[5,48,384]{2,1,0:T(8,128)(2,1)} %bitcast.7, bf16[48,640]{1,0:T(8,128)(2,1)} %qkv_h.1, bf16[48,384]{1,0:T(8,128)(2,1)} %outw_h.1, bf16[48,1024]{1,0:T(8,128)(2,1)} %head_h.1, f32[384]{0:T(512)} %cbias_h.1, f32[8,128]{1,0:T(8,128)} %bitcast.9, ...), custom_call_target="tpu_custom_call" | custom-call | tf_op jit(solution)/shard_map/pallas_call | solution.py:536
  77.8 1.4 %copy.10 = f32[8,1024]{1,0:T(8,128)} copy(f32[8,1024]{1,0:T(8,128)} %shard_map.82) | data formatting | bytes 65536

commit v5 on v4

--- a/solution.py
+++ b/solution.py
@@ -19,36 +19,39 @@
 D = 1536
 ROWS = 48
 COLS = 192
-WIDE = 640
+WIDE = 384
+WIDE2 = 256
 TAIL = 384
 KV = 256
 TRK = 512
 NZ = 8
 NY = 4
 
-QUICK = (
-    ((("O", 0), ("zp", "zm", "xp", "zp2", "zm2", "cp")),),
-    (
-        (("O", -1), ("cp",)),
-        (("O", 1), ("cp",)),
-        (("X", 0), ("zp", "zm", "cp")),
-        (("O", -2), ("zp", "xp", "cp")),
-        (("O", 2), ("zm", "cp")),
-    ),
-    (
-        (("O", -3), ("zp", "xp", "cp")),
-        (("O", 3), ("xp", "cp")),
-        (("X", 1), ("zm", "cp")),
-        (("X", -1), ("cp",)),
-        (("X", -2), ("cp",)),
-    ),
-    (
-        (("O", -4), ("xp", "cp")),
-        (("X", 2), ("cp",)),
-        (("X", 3), ("cp",)),
-        (("X", -3), ("cp",)),
-    ),
-    ((("X", -4), ("cp",)),),
+TREE = {
+    ("O", 0): ("zp2", "zm2", "xp"),
+    ("X", 0): ("zm",),
+    ("O", -2): ("xp", "zm", "zp"),
+    ("O", 2): ("zm", "xp", "zp"),
+    ("X", 1): (),
+    ("X", -2): ("zp2",),
+    ("O", -3): ("xp",),
+    ("O", -1): ("xp",),
+    ("X", 2): ("zm",),
+    ("O", 1): (),
+    ("O", 3): ("zm",),
+    ("X", -3): (),
+    ("X", 3): (),
+    ("X", -1): (),
+    ("O", -4): (),
+    ("X", -4): (),
+}
+EARLY = (
+    (0, "O", 0), (1, "O", 0), (2, "O", 0), (0, "X", 0), (1, "X", 0), (2, "X", 0), (0, "O", -2), (0, "O", 2),
+    (1, "O", -2), (1, "O", 2), (2, "O", -2), (2, "O", 2), (0, "X", 1), (1, "X", 1), (2, "X", 1), (0, "X", -2),
+    (0, "O", -3), (0, "O", -1), (0, "X", 2), (0, "O", 1), (1, "X", -2), (0, "O", 3), (1, "O", -3), (1, "X", 2),
+    (1, "O", -1), (1, "O", 1), (1, "O", 3), (2, "X", -2), (2, "O", -3), (2, "O", -1), (2, "X", 2), (2, "O", 1),
+    (2, "O", 3), (0, "X", -3), (0, "X", 3), (0, "X", -1), (1, "X", -3), (0, "O", -4), (0, "X", -4), (1, "X", -1),
+    (1, "X", 3), (1, "O", -4), (1, "X", -4), (2, "X", -3), (2, "X", 3), (2, "X", -1), (2, "O", -4), (2, "X", -4),
 )
 LEAN = (
     ((("O", 0), ("zp", "zm", "xp", "cp")),),
@@ -89,8 +92,8 @@
 def kernel(
     feats_h, conv_h, qkv_h, outw_h, head_h, cbias_h, hbias_h, exon_h,
     out,
-    feats, conv, qkv, cbias, hbias, exon, pa, pb, pk, ph, po,
-    wa, wb, wk, wh, wo, wo2, gx, ga, gr, ft, y, wqt, wkt, wht, hcol, trk, gmat, ex_out, ex_in, gs, gin,
+    feats, conv, qkv, cbias, hbias, exon, pa, pa2, pb, pk, ph, po,
+    wa, wa2, wb, wk, wh, wo, wo2, gx, ga, gr, ft, y, wqt, wkt, wht, hcol, trk, gmat, ex_out, ex_in, gs, gin,
     ring_r, ring_s, rsy, ssy, rsa, ssa, rsg, ssg, rse, sse, lsem,
 ):
     s = lax.axis_index("segment")
@@ -158,7 +161,10 @@
     for tap in range(TAPS):
         part = conv[tap].astype(F32)
         part = jnp.where(b == 0, part, pltpu.roll(part, COLS, 1))
-        pa[:, tap * 128 : tap * 128 + 128] = part[:, :128].astype(BF16)
+        if tap < 3:
+            pa[:, tap * 128 : tap * 128 + 128] = part[:, :128].astype(BF16)
+        else:
+            pa2[:, tap * 128 - 384 : tap * 128 - 256] = part[:, :128].astype(BF16)
         thin.append(part[:, 128:256])
     head_part = qkv[...].astype(F32)
     head_part = jnp.where(b == 0, head_part, pltpu.roll(head_part, 320, 1))
@@ -186,24 +192,29 @@
         def wait(win):
             remote(rows(win), rows(win), ring_s.at[index, 0], recv(win), to("cp")).wait_recv()
 
+        def take(code, names):
+            win = shard_win(code, c)
+            src = rows(win)
+            if code == ("O", 0):
+                src = rows(win) if own is None else own
+            else:
+                wait(win)
+            for name in names:
+                copy = remote(src, rows(win), ring_s.at[index, count[0]], recv(win), to(name))
+                count[0] += 1
+                copy.start()
+                tail.append(copy)
+
         def step(r):
-            for code, names in plan[r]:
-                win = shard_win(code, c)
-                src = rows(win)
-                if code == ("O", 0):
-                    src = rows(win) if own is None else own
-                else:
-                    wait(win)
-                for name in names:
-                    copy = remote(src, rows(win), ring_s.at[index, count[0]], recv(win), to(name))
-                    count[0] += 1
-                    copy.start()
-                    tail.append(copy)
+            if plan is None:
+                take(r, TREE[r] + ("cp",))
+            else:
+                for code, names in plan[r]:
+                    take(code, names)
 
         def rest():
-            for group in plan:
-                for code, names in group:
-                    wait(shard_win(code, 1 - c))
+            for code in TREE:
+                wait(shard_win(code, 1 - c))
 
         def flush():
             for copy in tail:
@@ -211,7 +222,7 @@
 
         keep = None
         if own is not None:
-            keep = pltpu.make_async_copy(own, rows(w), lsem.at[8 + index])
+            keep = pltpu.make_async_copy(own, rows(w), lsem.at[13 + index])
         return step, rest, flush, keep
 
     def gather(buf, index, lo, n):
@@ -261,8 +272,9 @@
 
         return start, first, second, third, flush
 
-    step_a, rest_a, flush_a, keep_a = ring(0, QUICK, pa, wa)
-    step_b, rest_b, flush_b, keep_b = ring(1, QUICK, pb, wb)
+    step_a, rest_a, flush_a, keep_a = ring(0, None, pa, wa)
+    step_a2, rest_a2, flush_a2, keep_a2 = ring(6, None, pa2, wa2)
+    step_b, rest_b, flush_b, keep_b = ring(1, None, pb, wb)
     step_k, rest_k, flush_k, keep_k = ring(2, LEAN, pk, wk)
     step_h, rest_h, flush_h, keep_h = ring(3, LEAN, ph, wh)
     step_o, rest_o, flush_o, _ = ring(4, LEAN, None, wo)
@@ -273,10 +285,15 @@
     start_v, first_v, second_v, third_v, flush_v = gather(ga, 2, 0, 96)
     start_w, first_w, second_w, third_w, flush_w = gather(ga, 3, 96, 96)
 
-    step_a(0)
-    step_b(0)
-    step_k(0)
+    early_steps = (step_a, step_a2, step_b)
+
+    def early(first, last):
+        for stream, kind, d in EARLY[first:last]:
+            early_steps[stream]((kind, d))
+
+    early(0, 3)
     keep_a.start()
+    keep_a2.start()
     keep_b.start()
     keep_k.start()
 
@@ -315,14 +332,7 @@
         lax.broadcasted_iota(jnp.int32, (BINS, BINS), 0) == lax.broadcasted_iota(jnp.int32, (BINS, BINS), 1)
     ).astype(F32).astype(BF16)
 
-    @pl.loop(0, D // BINS)
-    def _(n):
-        at = pl.ds(pl.multiple_of(n * BINS, BINS), BINS)
-        ft[:, at] = nt(eye, feats[at, :]).astype(BF16)
-
-    step_a(1)
-    step_b(1)
-    step_h(0)
+    early(3, 9)
 
     rows_id = lax.broadcasted_iota(jnp.int32, (512, 64), 0)
     owner = (
@@ -344,23 +354,38 @@
             total = total + jnp.where(inside, 1.0, 0.0)
         gmat[at, :] = total.astype(BF16)
 
-    for blk in range(2):
-        gene_bins(blk)
-    step_a(2)
-    step_b(2)
-    step_k(1)
-    step_h(1)
-    step_a(3)
-    step_b(3)
-    step_k(2)
+    gene_bins(0)
+    early(9, 14)
+    step_k(0)
+    early(14, 17)
+    gene_bins(1)
+    early(17, 25)
     wo_ready()
     step_o(0)
+
+    @pl.loop(0, D // BINS)
+    def _(n):
+        at = pl.ds(pl.multiple_of(n * BINS, BINS), BINS)
+        ft[:, at] = nt(eye, feats[at, :]).astype(BF16)
+
+    early(25, 31)
+    step_k(1)
+    early(31, 39)
     step_p(0)
-    step_a(4)
-    step_h(2)
-    step_b(4)
+    early(39, 40)
+    for blk in range(2, 4):
+        gene_bins(blk)
+    early(40, 43)
+    step_h(0)
+    early(43, 45)
+    step_o(1)
+    early(45, 46)
+    step_k(2)
+    early(46, 48)
     keep_a.wait()
+    keep_a2.wait()
     rest_a()
+    rest_a2()
 
     t_row = lax.broadcasted_iota(jnp.int32, (BINS, 128), 0)
 
@@ -379,17 +404,18 @@
     base2 = pl.multiple_of(q * COLS + 128, 64)
 
     for i in range(TAPS):
-        y[:, i * 128 : i * 128 + 128] = nn(ft[...], wa[:, i * 128 : i * 128 + 128])
+        part = wa[:, i * 128 : i * 128 + 128] if i < 3 else wa2[:, i * 128 - 384 : i * 128 - 256]
+        y[:, i * 128 : i * 128 + 128] = nn(ft[...], part)
     wide = shifted(y[:, 0:128], 0)
     for tap in range(1, TAPS):
         wide = wide + shifted(y[:, tap * 128 : tap * 128 + 128], tap)
     wide = gelu(wide + wide_bias).T
     gx[pl.ds(base, 128), :] = (feats[pl.ds(base, 128), :].astype(F32) + wide).astype(BF16)
     start_x()
+    step_h(1)
 
     keep_b.wait()
     rest_b()
-    step_o(1)
     pairs = [nn(ft[...], wb[:, i * 128 : i * 128 + 128]) for i in range(3)]
     even = shifted(pairs[0], 0) + shifted(pairs[1], 2) + shifted(pairs[2], 4)
     odd = shifted(pairs[0], 1) + shifted(pairs[1], 3)
@@ -397,22 +423,21 @@
     narrow = gelu(narrow + narrow_bias).T
     gx[pl.ds(base2, 64), :] = (feats[pl.ds(base2, 64), :].astype(F32) + narrow[:64]).astype(BF16)
     start_u()
+    step_o(2)
+    first_x()
     step_k(3)
     step_p(1)
-    first_x()
-    step_h(3)
-    for blk in range(2, 4):
-        gene_bins(blk)
     first_u()
-    step_o(2)
+    step_h(2)
     wqt[...] = nt(eye[:128, :128], wb[:, 256:384]).astype(BF16)
     second_x()
     step_k(4)
     second_u()
+    step_o(3)
     step_p(2)
     third_x()
     step_k(5)
-    step_o(3)
+    step_h(3)
     third_u()
     keep_k.wait()
     rest_k()
@@ -426,23 +451,23 @@
     ga[pl.ds(base, COLS), :] = nn(kv[64:256], prob).astype(BF16)
 
     start_v()
-    step_h(4)
+    start_w()
+    step_o(4)
     step_p(3)
-    start_w()
     for blk in range(4, 6):
         gene_bins(blk)
     first_v()
-    step_h(5)
-    step_o(4)
     first_w()
-    keep_h.wait()
-    rest_h()
-    step_p(4)
+    step_h(4)
     for blk in range(6, 8):
         gene_bins(blk)
     second_v()
     step_o(5)
+    step_p(4)
     second_w()
+    step_h(5)
+    keep_h.wait()
+    rest_h()
     for i in range(TRK // 256):
         wht[i * 256 : i * 256 + 256, :] = nt(eye, wh[:, i * 256 : i * 256 + 256]).astype(BF16)
     eye_f = (
@@ -453,6 +478,7 @@
         hcol[i * 128 : i * 128 + 128, :] = jnp.sum(jnp.where(eye_f, row, 0.0), axis=1, keepdims=True)
     step_p(5)
     flush_a()
+    flush_a2()
     flush_b()
     third_v()
     third_w()
@@ -535,7 +561,7 @@
     anywhere = pl.BlockSpec(memory_space=pltpu.HBM)
     return pl.pallas_call(
         kernel,
-        out_shape=jax.ShapeDtypeStruct((8, 1024), F32),
+        out_shape=vmem((8, 1024), F32),
         in_specs=[anywhere] * 8,
         out_specs=pl.BlockSpec(memory_space=pltpu.VMEM),
         scratch_shapes=[
@@ -546,11 +572,13 @@
             vmem((8, 128), F32),
             vmem((3, 8, 64), jnp.int32),
             vmem((ROWS, WIDE), BF16),
+            vmem((ROWS, WIDE2), BF16),
             vmem((ROWS, TAIL), BF16),
             vmem((ROWS, KV), BF16),
             vmem((ROWS, TRK), BF16),
             vmem((ROWS, 2 * COLS), BF16),
             vmem((D, WIDE), BF16),
+            vmem((D, WIDE2), BF16),
             vmem((D, TAIL), BF16),
             vmem((D, KV), BF16),
             vmem((D, TRK), BF16),
@@ -560,7 +588,7 @@
             vmem((D, BINS), BF16),
             vmem((D, BINS), BF16),
             vmem((BINS, D), BF16),
-            vmem((BINS, WIDE), F32),
+            vmem((BINS, WIDE + WIDE2), F32),
             vmem((128, D), BF16),
             vmem((KV, D), BF16),
             vmem((TRK, D), BF16),
@@ -571,8 +599,8 @@
             vmem((2, 32, 16, 128), BF16),
             vmem((32, 16, 256), BF16),
             vmem((32, 16, 256), BF16),
-            dma((6, 32)), dma((6, 34)), dma((4,)), dma((4,)),
-            dma((4, 8)), dma((4, 8)), dma((32,)), dma((32,)), dma((2,)), dma((2,)), dma((13,)),
+            dma((7, 32)), dma((7, 34)), dma((4,)), dma((4,)),
+            dma((4, 8)), dma((4, 8)), dma((32,)), dma((32,)), dma((2,)), dma((2,)), dma((20,)),
         ],
         compiler_params=pltpu.CompilerParams(
             collective_id=0, has_side_effects=True, vmem_limit_bytes=60 * 1024 * 1024

time: 79.4 us -> 78.9 us (level)
  no operation moved by 1% of the time
where the time goes in v5:
time: 78.9 us; the launch traced here: 78.8 us
  Pallas kernels  78.2 us (99%)
    pallas_call x1, Pallas kernels, local(): pl.pallas_call(kernel, out_shape=vmem((8, 1024), F32), in_specs=[anywhere...  78.2 us

profile of v5, /device:TPU:1, one launch (start us, length us, event | category | flops | bytes accessed | tf_op | source)
XLA Modules:
  0.0 78.8 jit_solution(14052578393090598164)
XLA Ops:
  0.0 78.2 %shard_map.82 = f32[8,1024]{1,0:T(8,128)S(1)} custom-call(bf16[1536,256]{1,0:T(8,128)(2,1)} %bitcast.6, bf16[5,48,384]{2,1,0:T(8,128)(2,1)} %bitcast.7, bf16[48,640]{1,0:T(8,128)(2,1)} %qkv_h.1, bf16[48,384]{1,0:T(8,128)(2,1)} %outw_h.1, bf16[48,1024]{1,0:T(8,128)(2,1)} %head_h.1, f32[384]{0:T(512)} %cbias_h.1, f32[8,128]{1,0:T(8,128)} %bitcast.9, ...), custom_call_target="tpu_custom_call" | custom-call | tf_op jit(solution)/shard_map/pallas_call | solution.py:562
  78.2 0.6 copy.10

commit v6 on v5

--- a/solution.py
+++ b/solution.py
@@ -360,9 +360,7 @@
     early(14, 17)
     gene_bins(1)
     early(17, 25)
-    wo_ready()
-    step_o(0)
-
+    step_h(0)
     @pl.loop(0, D // BINS)
     def _(n):
         at = pl.ds(pl.multiple_of(n * BINS, BINS), BINS)
@@ -371,17 +369,13 @@
     early(25, 31)
     step_k(1)
     early(31, 39)
+    step_h(1)
+    wo_ready()
+    early(39, 43)
+    step_o(0)
     step_p(0)
-    early(39, 40)
-    for blk in range(2, 4):
-        gene_bins(blk)
-    early(40, 43)
-    step_h(0)
-    early(43, 45)
-    step_o(1)
-    early(45, 46)
     step_k(2)
-    early(46, 48)
+    early(43, 48)
     keep_a.wait()
     keep_a2.wait()
     rest_a()
@@ -412,10 +406,10 @@
     wide = gelu(wide + wide_bias).T
     gx[pl.ds(base, 128), :] = (feats[pl.ds(base, 128), :].astype(F32) + wide).astype(BF16)
     start_x()
-    step_h(1)
 
     keep_b.wait()
     rest_b()
+    step_o(1)
     pairs = [nn(ft[...], wb[:, i * 128 : i * 128 + 128]) for i in range(3)]
     even = shifted(pairs[0], 0) + shifted(pairs[1], 2) + shifted(pairs[2], 4)
     odd = shifted(pairs[0], 1) + shifted(pairs[1], 3)
@@ -423,21 +417,22 @@
     narrow = gelu(narrow + narrow_bias).T
     gx[pl.ds(base2, 64), :] = (feats[pl.ds(base2, 64), :].astype(F32) + narrow[:64]).astype(BF16)
     start_u()
-    step_o(2)
-    first_x()
+    step_h(2)
     step_k(3)
     step_p(1)
+    first_x()
+    for blk in range(2, 4):
+        gene_bins(blk)
     first_u()
-    step_h(2)
+    step_o(2)
     wqt[...] = nt(eye[:128, :128], wb[:, 256:384]).astype(BF16)
     second_x()
     step_k(4)
+    step_h(3)
     second_u()
-    step_o(3)
     step_p(2)
     third_x()
     step_k(5)
-    step_h(3)
     third_u()
     keep_k.wait()
     rest_k()
@@ -452,22 +447,23 @@
 
     start_v()
     start_w()
-    step_o(4)
+    step_o(3)
+    step_h(4)
     step_p(3)
     for blk in range(4, 6):
         gene_bins(blk)
     first_v()
+    step_h(5)
+    step_o(4)
     first_w()
-    step_h(4)
+    keep_h.wait()
+    rest_h()
     for blk in range(6, 8):
         gene_bins(blk)
+    step_p(4)
     second_v()
     step_o(5)
-    step_p(4)
     second_w()
-    step_h(5)
-    keep_h.wait()
-    rest_h()
     for i in range(TRK // 256):
         wht[i * 256 : i * 256 + 256, :] = nt(eye, wh[:, i * 256 : i * 256 + 256]).astype(BF16)
     eye_f = (

time: 78.9 us -> 79.3 us (level)
  no operation moved by 1% of the time
where the time goes in v6:
time: 79.3 us; the launch traced here: 79.2 us
  Pallas kernels  78.6 us (99%)
    pallas_call x1, Pallas kernels, local(): pl.pallas_call(kernel, out_shape=vmem((8, 1024), F32), in_specs=[anywhere...  78.6 us

profile of v6, /device:TPU:1, one launch (start us, length us, event | category | flops | bytes accessed | tf_op | source)
XLA Modules:
  0.0 79.2 jit_solution(1091564234483905466)
XLA Ops:
  0.0 78.6 %shard_map.82 = f32[8,1024]{1,0:T(8,128)S(1)} custom-call(bf16[1536,256]{1,0:T(8,128)(2,1)} %bitcast.6, bf16[5,48,384]{2,1,0:T(8,128)(2,1)} %bitcast.7, bf16[48,640]{1,0:T(8,128)(2,1)} %qkv_h.1, bf16[48,384]{1,0:T(8,128)(2,1)} %outw_h.1, bf16[48,1024]{1,0:T(8,128)(2,1)} %head_h.1, f32[384]{0:T(512)} %cbias_h.1, f32[8,128]{1,0:T(8,128)} %bitcast.9, ...), custom_call_target="tpu_custom_call" | custom-call | tf_op jit(solution)/shard_map/pallas_call | solution.py:558
  78.6 0.6 copy.10

commit v7 on v4

--- a/solution.py
+++ b/solution.py
@@ -535,7 +535,7 @@
     anywhere = pl.BlockSpec(memory_space=pltpu.HBM)
     return pl.pallas_call(
         kernel,
-        out_shape=jax.ShapeDtypeStruct((8, 1024), F32),
+        out_shape=vmem((8, 1024), F32),
         in_specs=[anywhere] * 8,
         out_specs=pl.BlockSpec(memory_space=pltpu.VMEM),
         scratch_shapes=[

time: 79.4 us -> 77.9 us (0.981)
  no operation moved by 1% of the time
where the time goes in v7:
time: 77.9 us
  Pallas kernels  77.2 us (99%)
    pallas_call x1, Pallas kernels, local(): pl.pallas_call(kernel, out_shape=vmem((8, 1024), F32), in_specs=[anywhere...  77.2 us

profile of v7, /device:TPU:1, one launch (start us, length us, event | category | flops | bytes accessed | tf_op | source)
XLA Modules:
  0.0 77.9 jit_solution(17183850424907494472)
XLA Ops:
  0.0 77.2 %shard_map.82 = f32[8,1024]{1,0:T(8,128)S(1)} custom-call(bf16[1536,256]{1,0:T(8,128)(2,1)} %bitcast.6, bf16[5,48,384]{2,1,0:T(8,128)(2,1)} %bitcast.7, bf16[48,640]{1,0:T(8,128)(2,1)} %qkv_h.1, bf16[48,384]{1,0:T(8,128)(2,1)} %outw_h.1, bf16[48,1024]{1,0:T(8,128)(2,1)} %head_h.1, f32[384]{0:T(512)} %cbias_h.1, f32[8,128]{1,0:T(8,128)} %bitcast.9, ...), custom_call_target="tpu_custom_call" | custom-call | tf_op jit(solution)/shard_map/pallas_call | solution.py:536
  77.2 0.6 copy.10
